TPU v7x, 256 devices: a whole 4x4x8 slice. The times are simulated.
256 devices in a mesh: cells: 64 (over z, y, core), tm: 4 (over x).
Axes of the slice: x: 4, y: 4, z: 8, core: 2. Of those that a mesh axis runs over, the one named last changes fastest.
Arguments:
- attitude: float32 [4, 65536], P(None, ('cells', 'tm')), may hold values from -6 to 6
- star_partials: float32 [5, 64, 131072], P(None, None, ('cells', 'tm')), may hold values from -6 to 6
- attitude_partials: float32 [4, 64, 131072], P(None, None, ('cells', 'tm')), may hold values from -6 to 6
- observed: float32 [64, 131072], P(None, ('cells', 'tm')), may hold values from -6 to 6
- phase: float32 [64, 131072], P(None, ('cells', 'tm')), may hold values from 0 to 1
- knot_offset: int32 [64, 131072], P(None, ('cells', 'tm')), may hold values from 0 to 12
- cell_counts: int32 [1024], P(('cells', 'tm')), may hold values from 40 to 64, as said below
- interval_owner: int32 [1024, 64, 1], P(('cells', 'tm')), may hold values from 0 to 255; in each aligned block of 256 rows (0 to 255, 256 to 511, ..., all dimensions but the last counted through in order) at most 2 rows name the same one
- block_slot: int32 [1024, 64], P(('cells', 'tm')), may hold values from 0 to 15
Outputs:
- star_step: float32 [5, 131072], P(None, ('cells', 'tm'))
- attitude_step: float32 [4, 65536], P(None, ('cells', 'tm'))
Inputs may be any that keep to these rules, and one draw needn't show every extreme that they name: `interval_owner`: among the 256 transits of the cells of one device no owner is named more than 2 times, and in every draw some owner is named exactly 2 times by the transits of some device. Transits that are not live are listed too. `cell_counts`: some cell has all 64 transits live in every draw.
All inputs are finite; a program needn't handle non-finite values.
Results may differ from a plain program's by a relative error of at most 0.0003.
Values sent between devices are 32-bit elements; how exact they have to be, the bound alone decides.
A program may use at most 128 MiB of HBM per device.

v0:
```python
import jax
import jax.numpy as jnp
from jax import lax
from jax.sharding import PartitionSpec as P

CS = 128
KB = 16
ITERS = 6


smoothing = 16.0
damping = 2.0
relaxation = 0.5
star_prior = 1.0
highest = lax.Precision.HIGHEST


def padded_2(shard, sides, width):
    for axis, dim in sides:
        size, length = (lax.axis_size(axis), shard.shape[dim])
        up = [(i, (i + 1) % size) for i in range(size - 1)]
        down = [(j, i) for i, j in up]
        last = lax.slice_in_dim(shard, length - width, length, axis=dim)
        leading = lax.slice_in_dim(shard, 0, width, axis=dim)
        before = lax.ppermute(last, axis, up)
        after = lax.ppermute(leading, axis, down)
        shard = jnp.concatenate([before, shard, after], axis=dim)
    return shard


def spline_basis(phase):
    square = phase * phase
    cube = square * phase
    rest = 1.0 - phase
    return (
        rest * rest * rest / 6.0,
        (3.0 * cube - 6.0 * square + 4.0) / 6.0,
        (-3.0 * cube + 3.0 * square + 3.0 * phase + 1.0) / 6.0,
        cube / 6.0,
    )


def design_rows(phase, knot_offset, partials, live):
    knots = lax.broadcasted_iota(jnp.int32, (KB, 1), 0)
    basis = spline_basis(phase)
    spread = jnp.zeros(phase.shape[:-1] + (KB, phase.shape[-1]), jnp.float32)
    for order in range(4):
        hit = knots == knot_offset[..., None, :] + order
        spread = spread + jnp.where(hit, basis[order][..., None, :], 0.0)
    spread = spread * live[..., None, None]
    return jnp.moveaxis(partials, 0, -2)[..., :, None, :] * spread[..., None, :, :]


def cholesky_factor(matrix, size):
    lower = [[None for column in range(size)] for row in range(size)]
    for column in range(size):
        total = matrix[column][column]
        for inner in range(column):
            total = total - lower[column][inner] * lower[column][inner]
        pivot = jnp.sqrt(total)
        lower[column][column] = pivot
        for row in range(column + 1, size):
            accum = matrix[row][column]
            for inner in range(column):
                accum = accum - lower[row][inner] * lower[column][inner]
            lower[row][column] = accum / pivot
    return lower


def cholesky_solve(lower, rhs, size):
    forward = []
    for row in range(size):
        accum = rhs[row]
        for inner in range(row):
            accum = accum - lower[row][inner] * forward[inner]
        forward.append(accum / lower[row][row])
    answer = [None for row in range(size)]
    for row in reversed(range(size)):
        accum = forward[row]
        for inner in range(row + 1, size):
            accum = accum - lower[inner][row] * answer[inner]
        answer[row] = accum / lower[row][row]
    return answer


def star_update(partials, first, live):
    normal = [
        [
            jnp.sum(live * partials[row] * partials[column], axis=0)
            + (star_prior if row == column else 0.0)
            for column in range(5)
        ]
        for row in range(5)
    ]
    rhs = [jnp.sum(partials[row] * first, axis=0) for row in range(5)]
    lower = cholesky_factor(normal, 5)
    step = cholesky_solve(lower, rhs, 5)
    fitted = partials[0] * step[0]
    for row in range(1, 5):
        fitted = fitted + partials[row] * step[row]
    return (jnp.stack(step), first - live * fitted)


def dense_to_band(dense):
    pieces = []
    for shift in range(4):
        diagonal = jnp.diagonal(dense, offset=shift, axis1=2, axis2=4)
        filler = jnp.zeros(diagonal.shape[:-1] + (shift,), jnp.float32)
        pieces.append(jnp.concatenate([diagonal, filler], axis=-1))
    return jnp.stack(pieces, axis=-2)


def band_apply(band, vector):
    result = jnp.einsum("bmna,nba->mba", band[:, :, :, 0, :], vector, precision=highest)
    for shift in range(1, 4):
        filler = jnp.zeros(vector.shape[:-1] + (shift,), jnp.float32)
        ahead = jnp.concatenate([vector[..., shift:], filler], axis=-1)
        result = result + jnp.einsum(
            "bmna,nba->mba", band[:, :, :, shift, :], ahead, precision=highest
        )
        lagged = jnp.einsum("bnma,nba->mba", band[:, :, :, shift, :], vector, precision=highest)
        result = result + jnp.concatenate([filler, lagged[..., : KB - shift]], axis=-1)
    return result


def diagonal_factor(band):
    shifted = 2.0 * smoothing + damping
    entries = [
        [band[:, row, column, 0, :] + (shifted if row == column else 0.0) for column in range(4)]
        for row in range(4)
    ]
    return cholesky_factor(entries, 4)


def sweep(band, lower, gradient, solution, padded):
    count = band.shape[0]
    applied = band_apply(band, solution.reshape(4, count, KB))
    regular = smoothing * (2.0 * solution - padded[:, :-2] - padded[:, 2:]) + damping * solution
    misfit = gradient - applied - regular.reshape(4, count, KB)
    correction = cholesky_solve(lower, [misfit[row] for row in range(4)], 4)
    return solution + relaxation * jnp.stack(correction).reshape(4, count * KB)


def cell_work(items):
    cell_phase, cell_offset, cell_axis, cell_star, cell_observed, cell_live, cell_values = items
    rows = design_rows(cell_phase, cell_offset, cell_axis, cell_live)
    predicted = jnp.einsum("tmas,tma->ts", rows, cell_values, precision=highest)
    first = cell_live[:, None] * cell_observed - predicted
    step, second = star_update(cell_star, first, cell_live[:, None])
    gradient = jnp.einsum("tmas,ts->tma", rows, second, precision=highest)
    flat = rows.reshape(rows.shape[0], 4 * KB, rows.shape[-1])
    normal = jnp.einsum("tis,tks->tik", flat, flat, precision=highest).reshape(
        rows.shape[0], 16 * KB * KB
    )
    return (step, normal, gradient.reshape(rows.shape[0], 4 * KB))


def per_device(
    attitude,
    star_partials,
    attitude_partials,
    observed,
    phase,
    knot_offset,
    cell_counts,
    interval_owner,
    block_slot,
):
    cell_groups = lax.axis_size("cells")
    time_groups = lax.axis_size("tm")
    devices = cell_groups * time_groups
    cells_here = cell_counts.shape[0]
    transits = observed.shape[0]
    blocks_here = attitude.shape[1] // KB
    total = cells_here * transits
    capacity = max(2, 3 * total // (2 * devices))
    owners = interval_owner.reshape(total)
    slots = block_slot.reshape(total)
    order = lax.broadcasted_iota(jnp.int32, (total, total), 0)
    other = lax.broadcasted_iota(jnp.int32, (total, total), 1)
    same = (owners[:, None] == owners[None, :]) & (other < order)
    rank = jnp.sum(same.astype(jnp.int32), axis=1)
    position = owners * capacity + rank
    requests = jnp.zeros((devices * capacity,), jnp.int32).at[position].set(slots)
    requested = lax.all_to_all(
        lax.all_to_all(
            requests.reshape(cell_groups, time_groups, capacity),
            "cells",
            split_axis=0,
            concat_axis=0,
            tiled=True,
        ),
        "tm",
        split_axis=1,
        concat_axis=1,
        tiled=True,
    )
    whole = lax.all_gather(attitude, ("cells", "tm"), axis=1, tiled=True)
    global_ids = owners * blocks_here + slots
    values = whole.reshape(4, -1, KB)[:, global_ids, :].transpose(1, 0, 2)
    transit = lax.broadcasted_iota(jnp.int32, (cells_here, transits), 1)
    live = jnp.where(transit < cell_counts[:, None], 1.0, 0.0).astype(jnp.float32)
    items = (
        phase.reshape(transits, cells_here, CS).transpose(1, 0, 2),
        knot_offset.reshape(transits, cells_here, CS).transpose(1, 0, 2),
        attitude_partials.reshape(4, transits, cells_here, CS).transpose(2, 0, 1, 3),
        star_partials.reshape(5, transits, cells_here, CS).transpose(2, 0, 1, 3),
        observed.reshape(transits, cells_here, CS).transpose(1, 0, 2),
        live,
        values.reshape(cells_here, transits, 4, KB),
    )
    steps, normals, gradients = lax.map(cell_work, items)
    payload = normals.reshape(total, normals.shape[-1])
    gradient_rows = gradients.reshape(total, 4 * KB)
    outgoing = (
        jnp.zeros((devices * capacity, payload.shape[1]), jnp.float32).at[position].set(payload)
    )
    outgoing_grad = (
        jnp.zeros((devices * capacity, 4 * KB), jnp.float32).at[position].set(gradient_rows)
    )
    arrived, arrived_grad = (
        lax.all_to_all(
            lax.all_to_all(
                outgoing.reshape(cell_groups, time_groups, capacity, payload.shape[1]),
                "cells",
                split_axis=0,
                concat_axis=0,
                tiled=True,
            ),
            "tm",
            split_axis=1,
            concat_axis=1,
            tiled=True,
        ),
        lax.all_to_all(
            lax.all_to_all(
                outgoing_grad.reshape(cell_groups, time_groups, capacity, 4 * KB),
                "cells",
                split_axis=0,
                concat_axis=0,
                tiled=True,
            ),
            "tm",
            split_axis=1,
            concat_axis=1,
            tiled=True,
        ),
    )
    member_rows = lax.broadcasted_iota(jnp.int32, (blocks_here, devices * capacity), 0)
    member = (member_rows == requested.reshape(1, devices * capacity)).astype(jnp.float32)
    block_normal = jnp.dot(
        member,
        arrived.reshape(devices * capacity, payload.shape[1]),
        precision=highest,
        preferred_element_type=jnp.float32,
    )
    block_grad = jnp.dot(
        member,
        arrived_grad.reshape(devices * capacity, 4 * KB),
        precision=highest,
        preferred_element_type=jnp.float32,
    )
    band = dense_to_band(block_normal.reshape(blocks_here, 4, KB, 4, KB))
    gradient = block_grad.reshape(blocks_here, 4, KB).transpose(1, 0, 2)
    lower = diagonal_factor(band)
    solution = jnp.zeros((4, blocks_here * KB), jnp.float32)
    for index in range(ITERS):
        padded = padded_2(solution, ((("cells", "tm"), 1),), 1)
        solution = sweep(band, lower, gradient, solution, padded)
    star_step = steps.transpose(1, 0, 2).reshape(5, cells_here * CS)
    return (star_step, solution)


def solution(mesh):
    placed = (
        P(None, ("cells", "tm")),
        P(None, None, ("cells", "tm")),
        P(None, None, ("cells", "tm")),
        P(None, ("cells", "tm")),
        P(None, ("cells", "tm")),
        P(None, ("cells", "tm")),
        P(("cells", "tm")),
        P(("cells", "tm"), None, None),
        P(("cells", "tm"), None),
    )
    return jax.shard_map(
        per_device,
        mesh=mesh,
        in_specs=placed,
        out_specs=(P(None, ("cells", "tm")), P(None, ("cells", "tm"))),
        check_vma=False,
    )
```

profile of v0, /device:TPU:127, one launch (start us, length us, event | category | flops | bytes accessed | tf_op | source)
XLA Modules:
  0.0 741.4 jit_solution(1246843753524124529)
XLA Ops:
  14.2 10.9 %all-to-all-start = ((s32[64,4,2]{1,2,0:T(2,128)}), s32[64,4,2]{1,2,0:T(2,128)S(1)}, u32[]{:S(2)}, u32[]{:S(2)}) async-start(s32[64,4,2]{1,2,0:T(2,128)} %copy.75), calls=%async_computation | async-start | bytes 131072 | tf_op jit(solution)/shard_map/all_to_all | solution.py:186
  39.9 75.8 %all-gather.2.cloned.1.call-done = f32[4,65536]{1,0:T(4,128)} async-done(((f32[4,256]{1,0:T(4,128)}), f32[4,65536]{1,0:T(4,128)}) %all-gather.2.cloned.1.call-update) | async-done | bytes 1048592 | tf_op jit(solution)/shard_map/all_gather | solution.py:198
  115.7 7.3 reshape.1760
  123.1 11.8 %copy.67 = f32[4,4096,16]{2,0,1:T(4,128)} copy(f32[4,4096,16]{2,1,0:T(8,128)} %reshape.1760) | data formatting | bytes 2097152 | tf_op jit(solution)/shard_map/reshape | solution.py:200
  139.5 125.9 %while.14 = (s32[]{:T(128)}, f32[4,5,128]{2,1,0:T(8,128)}, f32[4,64,4096]{2,1,0:T(8,128)}, f32[4,64,64]{2,1,0:T(8,128)}, f32[4,5,64,128]{3,0,2,1:T(4,128)}, /*in...) while((s32[]{:T(128)}, f32[4,5,128]{2,1,0:T(8,128)}, ...), condition=%wide.region_21.22_spmd, body=%wide.region_0.21_spmd.sunk | while | flops 419069696 | bytes 14432589 | solution.py:212
  147.6 14.7 %fusion.269 = f32[64,1,4,16]{3,1,2,0:T(1,128)S(1)} fusion(f32[64,128,1,1]{1,2,3,0:T(1,128)S(1)} %bitcast.973, f32[64,16,128]{2,1,0:T(8,128)S(1)} %add_multiply_fusion.2, f32[64,4,128]{2,1,0:T(4,128)S(1)} %bitcast.953), kind=kOutput, calls=%fused_computation.8.clone.1 | convolution fusion | flops 6815744 | bytes 704512 | tf_op jit(solution)/shard_map/while/body/eval_jaxpr/tmas,ts->tma/dot_general | solution.py:150
  178.8 14.7 %fusion.269 = f32[64,1,4,16]{3,1,2,0:T(1,128)S(1)} fusion(f32[64,128,1,1]{1,2,3,0:T(1,128)S(1)} %bitcast.973, f32[64,16,128]{2,1,0:T(8,128)S(1)} %add_multiply_fusion.2, f32[64,4,128]{2,1,0:T(4,128)S(1)} %bitcast.953), kind=kOutput, calls=%fused_computation.8.clone.1 | convolution fusion | flops 6815744 | bytes 704512 | tf_op jit(solution)/shard_map/while/body/eval_jaxpr/tmas,ts->tma/dot_general | solution.py:150
  210.2 14.7 %fusion.269 = f32[64,1,4,16]{3,1,2,0:T(1,128)S(1)} fusion(f32[64,128,1,1]{1,2,3,0:T(1,128)S(1)} %bitcast.973, f32[64,16,128]{2,1,0:T(8,128)S(1)} %add_multiply_fusion.2, f32[64,4,128]{2,1,0:T(4,128)S(1)} %bitcast.953), kind=kOutput, calls=%fused_computation.8.clone.1 | convolution fusion | flops 6815744 | bytes 704512 | tf_op jit(solution)/shard_map/while/body/eval_jaxpr/tmas,ts->tma/dot_general | solution.py:150
  241.5 14.7 %fusion.269 = f32[64,1,4,16]{3,1,2,0:T(1,128)S(1)} fusion(f32[64,128,1,1]{1,2,3,0:T(1,128)S(1)} %bitcast.973, f32[64,16,128]{2,1,0:T(8,128)S(1)} %add_multiply_fusion.2, f32[64,4,128]{2,1,0:T(4,128)S(1)} %bitcast.953), kind=kOutput, calls=%fused_computation.8.clone.1 | convolution fusion | flops 6815744 | bytes 704512 | tf_op jit(solution)/shard_map/while/body/eval_jaxpr/tmas,ts->tma/dot_general | solution.py:150
  267.8 8.8 %all-to-all-start.2 = ((f32[64,1,512]{2,1,0:T(1,128)}), f32[64,1,512]{2,1,0:T(1,128)S(1)}, u32[]{:S(2)}, u32[]{:S(2)}) async-start(f32[64,1,512]{2,1,0:T(1,128)} %reshape.1951), calls=%async_computation.2 | async-start | bytes 262144 | tf_op jit(solution)/shard_map/all_to_all | solution.py:236
  276.7 8.2 %scatter_custom_fusion.2 = f32[512,4096]{1,0:T(8,128)} fusion(s32[256]{0:T(256)} %bitcast.1001, f32[256,4096]{1,0:T(8,128)} %bitcast.1002, f32[]{:T(128)} %constant.54.clone.1), kind=kCustom, calls=%fused_computation.167 | custom fusion | bytes 8389120 | tf_op jit(solution)/shard_map/scatter | solution.py:216
  284.9 10.6 %reshape.1770 = f32[64,4,2,4096]{3,2,1,0:T(2,128)} reshape(f32[512,4096]{1,0:T(8,128)} %scatter_custom_fusion.2) | data formatting | bytes 16777216 | tf_op jit(solution)/shard_map/reshape | solution.py:224
  295.5 10.5 %all-to-all-start.4 = ((f32[64,4,2,4096]{3,2,1,0:T(2,128)}), f32[64,4,2,4096]{3,2,1,0:T(2,128)}, u32[]{:S(2)}, u32[]{:S(2)}) async-start(f32[64,4,2,4096]{3,2,1,0:T(2,128)} %reshape.1770), calls=%async_computation.4 | async-start | bytes 16777216 | tf_op jit(solution)/shard_map/all_to_all | solution.py:223
  308.6 178.9 %all-to-all-done.4 = f32[64,4,2,4096]{3,2,1,0:T(2,128)} async-done(((f32[64,4,2,4096]{3,2,1,0:T(2,128)}), f32[64,4,2,4096]{3,2,1,0:T(2,128)}, u32[]{:S(2)}, u32[]{:S(2)}) %all-to-all-start.4) | async-done | bytes 8388640 | tf_op jit(solution)/shard_map/all_to_all | solution.py:223
  491.8 7.4 copy.83
  510.2 85.5 %collective-permute-done = f32[4,1]{1,0:T(4,128)S(1)} collective-permute-done((f32[4,1]{1,0:T(4,128)S(1)}, f32[4,1]{1,0:T(4,128)S(1)}, u32[]{:S(2)}, u32[]{:S(2)}) %collective-permute-start) | collective-permute-done | bytes 48 | tf_op jit(solution)/shard_map/ppermute | solution.py:25
  599.8 7.6 %copy.84 = f32[64,4,2,4096]{3,2,1,0:T(2,128)} copy(f32[64,4,2,4096]{3,2,0,1:T(2,128)} %all-to-all-done.5) | data formatting | bytes 16777216 | tf_op jit(solution)/shard_map/all_to_all | solution.py:222
  607.4 10.9 %reshape.1771 = f32[512,4096]{1,0:T(8,128)} reshape(f32[64,4,2,4096]{3,2,1,0:T(2,128)} %copy.84) | data formatting | bytes 16777216 | tf_op jit(solution)/shard_map/reshape | solution.py:253
  618.3 9.0 %copy.85 = f32[4096,512]{1,0:T(8,128)} copy(f32[4096,512]{0,1:T(8,128)} %bitcast.915) | data formatting | bytes 16777216 | tf_op jit(solution)/shard_map/dot_general | solution.py:251
  627.3 17.0 %convolution_bitcast_fusion = f32[16,4,4,16,16]{4,0,2,3,1:T(8,128)S(1)} fusion(f32[4,16,4,16,512]{4,3,2,1,0:T(8,128)} %bitcast.914, s32[512]{0:T(512)S(1)} %eq.99), kind=kOutput, calls=%fused_computation.169 | convolution fusion | flops 402661376 | bytes 8652800 | tf_op jit(solution)/shard_map/dot_general | solution.py:251
  665.9 8.4 %collective-permute-done.3 = f32[4,1]{1,0:T(4,128)S(1)} collective-permute-done((f32[4,1]{1,0:T(4,128)S(1)}, f32[4,1]{1,0:T(4,128)S(1)}, u32[]{:S(2)}, u32[]{:S(2)}) %collective-permute-start.3) | collective-permute-done | bytes 48 | tf_op jit(solution)/shard_map/ppermute | solution.py:26
  682.0 7.0 collective-permute-done.5
  711.3 7.0 collective-permute-done.9
  726.0 7.0 collective-permute-done.11
  (517 shorter events, 176.2 us)
Async XLA Ops:
  7.2 108.6 %all-gather.2.cloned.1.call-start = ((), (), s32[]{:S(2)}) async-start(), calls=%async_computation.6 | async-start | bytes 1052672 | tf_op jit(solution)/shard_map/all_gather | solution.py:198
  14.2 20.7 %all-to-all-start = ((s32[64,4,2]{1,2,0:T(2,128)}), s32[64,4,2]{1,2,0:T(2,128)S(1)}, u32[]{:S(2)}, u32[]{:S(2)}) async-start(s32[64,4,2]{1,2,0:T(2,128)} %copy.75), calls=%async_computation | async-start | bytes 131072 | tf_op jit(solution)/shard_map/all_to_all | solution.py:186
  35.7 232.2 %all-to-all-start.1 = ((s32[4,1,128]{2,1,0:T(1,128)}), s32[4,1,128]{2,1,0:T(1,128)}, u32[]{:S(2)}, u32[]{:S(2)}) async-start(s32[4,1,128]{2,1,0:T(1,128)} %reshape.1949), calls=%async_computation.1 | async-start | bytes 4096 | tf_op jit(solution)/shard_map/all_to_all | solution.py:185
  146.8 0.6 copy-start.1
  146.9 0.6 copy-start.7
  178.1 0.6 copy-start.1
  240.7 0.6 copy-start.1
  240.8 0.6 copy-start.7
  267.8 27.6 %all-to-all-start.2 = ((f32[64,1,512]{2,1,0:T(1,128)}), f32[64,1,512]{2,1,0:T(1,128)S(1)}, u32[]{:S(2)}, u32[]{:S(2)}) async-start(f32[64,1,512]{2,1,0:T(1,128)} %reshape.1951), calls=%async_computation.2 | async-start | bytes 262144 | tf_op jit(solution)/shard_map/all_to_all | solution.py:236
  295.5 192.1 %all-to-all-start.4 = ((f32[64,4,2,4096]{3,2,1,0:T(2,128)}), f32[64,4,2,4096]{3,2,1,0:T(2,128)}, u32[]{:S(2)}, u32[]{:S(2)}) async-start(f32[64,4,2,4096]{3,2,1,0:T(2,128)} %reshape.1770), calls=%async_computation.4 | async-start | bytes 16777216 | tf_op jit(solution)/shard_map/all_to_all | solution.py:223
  487.6 11.6 %all-to-all-start.3 = ((f32[4,1,8192]{2,1,0:T(1,128)}), f32[4,1,8192]{2,1,0:T(1,128)S(1)}, u32[]{:S(2)}, u32[]{:S(2)}) async-start(f32[4,1,8192]{2,1,0:T(1,128)} %reshape.1953), calls=%async_computation.3 | async-start | bytes 262144 | tf_op jit(solution)/shard_map/all_to_all | solution.py:235
  499.2 100.6 %all-to-all-start.5 = ((f32[64,4,2,4096]{3,2,0,1:T(2,128)}), f32[64,4,2,4096]{3,2,0,1:T(2,128)}, u32[]{:S(2)}, u32[]{:S(2)}) async-start(f32[64,4,2,4096]{3,2,0,1:T(2,128)} %copy.83), calls=%async_computation.5 | async-start | bytes 16777216 | tf_op jit(solution)/shard_map/all_to_all | solution.py:222
  504.9 90.9 %collective-permute-start = (f32[4,1]{1,0:T(4,128)S(1)}, f32[4,1]{1,0:T(4,128)S(1)}, u32[]{:S(2)}, u32[]{:S(2)}) collective-permute-start(f32[4,1]{1,0:T(4,128)S(1)} %broadcast.741), channel_id=1, source_target_pairs={{0,1},{1,2},{2,3},{3,4},{4,5},{5,6},{6,7},{7,8},{8,9},{9,10},{10,1... | collective-permute-start | bytes 56 | tf_op jit(solution)/shard_map/ppermute | solution.py:25
  508.2 87.5 %collective-permute-start.1 = (f32[4,1]{1,0:T(4,128)S(1)}, f32[4,1]{1,0:T(4,128)S(1)}, u32[]{:S(2)}, u32[]{:S(2)}) collective-permute-start(f32[4,1]{1,0:T(4,128)S(1)} %broadcast.741), channel_id=1, source_target_pairs={{1,0},{2,1},{3,2},{4,3},{5,4},{6,5},{7,6},{8,7},{9,8},{10,9},{11,1... | collective-permute-start | bytes 56 | tf_op jit(solution)/shard_map/ppermute | solution.py:26
  658.6 7.3 collective-permute-start.2
  664.0 10.3 %collective-permute-start.3 = (f32[4,1]{1,0:T(4,128)S(1)}, f32[4,1]{1,0:T(4,128)S(1)}, u32[]{:S(2)}, u32[]{:S(2)}) collective-permute-start(f32[4,1]{1,0:T(4,128)S(1)} %get-tuple-element.277), channel_id=1, source_target_pairs={{1,0},{2,1},{3,2},{4,3},{5,4},{6,5},{7,6},{8,7},{9,8},{10,9},{11,1... | collective-permute-start | bytes 56 | tf_op jit(solution)/shard_map/ppermute | solution.py:26
  676.7 5.3 collective-permute-start.4
  678.6 10.3 %collective-permute-start.5 = (f32[4,1]{1,0:T(4,128)S(1)}, f32[4,1]{1,0:T(4,128)S(1)}, u32[]{:S(2)}, u32[]{:S(2)}) collective-permute-start(f32[4,1]{1,0:T(4,128)S(1)} %get-tuple-element.275), channel_id=1, source_target_pairs={{1,0},{2,1},{3,2},{4,3},{5,4},{6,5},{7,6},{8,7},{9,8},{10,9},{11,1... | collective-permute-start | bytes 56 | tf_op jit(solution)/shard_map/ppermute | solution.py:26
  691.3 5.5 collective-permute-start.6
  693.3 10.3 %collective-permute-start.7 = (f32[4,1]{1,0:T(4,128)S(1)}, f32[4,1]{1,0:T(4,128)S(1)}, u32[]{:S(2)}, u32[]{:S(2)}) collective-permute-start(f32[4,1]{1,0:T(4,128)S(1)} %get-tuple-element.273), channel_id=1, source_target_pairs={{1,0},{2,1},{3,2},{4,3},{5,4},{6,5},{7,6},{8,7},{9,8},{10,9},{11,1... | collective-permute-start | bytes 56 | tf_op jit(solution)/shard_map/ppermute | solution.py:26
  706.0 5.3 collective-permute-start.8
  708.0 10.3 %collective-permute-start.9 = (f32[4,1]{1,0:T(4,128)S(1)}, f32[4,1]{1,0:T(4,128)S(1)}, u32[]{:S(2)}, u32[]{:S(2)}) collective-permute-start(f32[4,1]{1,0:T(4,128)S(1)} %get-tuple-element.271), channel_id=1, source_target_pairs={{1,0},{2,1},{3,2},{4,3},{5,4},{6,5},{7,6},{8,7},{9,8},{10,9},{11,1... | collective-permute-start | bytes 56 | tf_op jit(solution)/shard_map/ppermute | solution.py:26
  720.7 5.3 collective-permute-start.10
  722.7 10.3 %collective-permute-start.11 = (f32[4,1]{1,0:T(4,128)S(1)}, f32[4,1]{1,0:T(4,128)S(1)}, u32[]{:S(2)}, u32[]{:S(2)}) collective-permute-start(f32[4,1]{1,0:T(4,128)S(1)} %get-tuple-element.269), channel_id=1, source_target_pairs={{1,0},{2,1},{3,2},{4,3},{5,4},{6,5},{7,6},{8,7},{9,8},{10,9},{11,1... | collective-permute-start | bytes 56 | tf_op jit(solution)/shard_map/ppermute | solution.py:26
  (60 other events, 34.1 us)
Sparse Core Ops, SparseCore 0:
  11.7 103.9 all-gather.1
where the time goes:
time: 751 us; the launch traced here: 741 us
  waiting for transfers between devices  377 us (50%)
  local copies, waits for them, and re-layouts  148 us (20%)
  matrix products  97.9 us (13%)
  starting transfers between devices  78.2 us (10%)
  other arithmetic  23.7 us (3%)
  between operations  15.1 us (2%)
    all_to_all x1, waiting for transfers between devices, per_device(): lax.all_to_all(outgoing.reshape(cell_groups, time_groups, capacity, paylo...  179 us
    ppermute x6, waiting for transfers between devices, padded_2(): before = lax.ppermute(last, axis, up)  85.5 us
    all_gather x1, waiting for transfers between devices, per_device(): whole = lax.all_gather(attitude, ('cells', 'tm'), axis=1, tiled=True)  75.8 us
    dot_general x4, matrix products, cell_work(): gradient = jnp.einsum('tmas,ts->tma', rows, second, precision=highest)  58.7 us
    ppermute x6, waiting for transfers between devices, padded_2(): after = lax.ppermute(leading, axis, down)  36.1 us
    reshape x2, local copies, waits for them, and re-layouts, per_device(): values = whole.reshape(4, -1, KB)[:, global_ids, :].transpose(1, 0, 2)  19.2 us
    ppermute x6, starting transfers between devices, padded_2(): after = lax.ppermute(leading, axis, down)  17.4 us
    dot_general x1, matrix products, per_device(): jnp.dot(member, arrived.reshape(devices * capacity, payload.shape[1]), pr...  17 us
  transfers between devices with their start and end apart: 19, of which 8 were waited for; matrix products, arithmetic and copies ran while one was open for 27% of the time, Pallas kernels for 0%

commit v1 on v0

v1 whole, which is shorter than its diff:
```python
import functools

import jax
import jax.numpy as jnp
from jax import lax
from jax.experimental import pallas as pl
from jax.experimental.pallas import tpu as pltpu
from jax.sharding import PartitionSpec as P

NT, CS, KB, ITERS = 64, 128, 16, 6
NX, NY, NZ, NC = 4, 4, 8, 2
NP = NX * NY
DEV = NP * NZ * NC
QIN = NZ * NC
CELLS_HERE = 4
TR = CELLS_HERE * NT
ID_LANE = 63
MESH = pl.DeviceIdType.MESH
f32, bf16 = jnp.float32, jnp.bfloat16
PAIRS = [(m, n) for m in range(4) for n in range(m, 4)]
PAIR_OF = {pair: i for i, pair in enumerate(PAIRS)}
PAIR_ROW = [i if i < 5 else i + 3 for i in range(10)]
SHIFTS = [(t, i) for t in range(4) for i in range(4 - t)]
SHIFT_OF = {pair: i for i, pair in enumerate(SHIFTS)}
VMEM = pl.BlockSpec(memory_space=pltpu.VMEM)
SMEM = pl.BlockSpec(memory_space=pltpu.SMEM)


def place():
    cells, x = lax.axis_index("cells"), lax.axis_index("tm")
    z, y, c = cells // (NY * NC), (cells // NC) % NY, cells % NC
    return x, y, z, c


def device(x, y, z, c):
    return ((z * NY + y) * NC + c, x)


def remote(src, dst, send, recv, target):
    return pltpu.make_async_remote_copy(
        src_ref=src, dst_ref=dst, send_sem=send, recv_sem=recv, device_id=target, device_id_type=MESH
    )


def plane_peers(x, y, z, c):
    here = x * NY + y
    peers = []
    for i in range(1, NP):
        there = (here + i) % NP
        peers.append((there, device(there // NY, there % NY, z, c)))
    return peers


def column_peers(x, y, z, c):
    return [((z + i) % NZ, device(x, y, (z + i) % NZ, c)) for i in range(1, NZ)]


def greet(targets):
    barrier = pltpu.get_barrier_semaphore()
    for target in targets:
        pl.semaphore_signal(barrier, inc=1, device_id=target, device_id_type=MESH)
    pl.semaphore_wait(barrier, len(targets))


def gather_kernel(att_ref, out_ref, zs, zr, ps, pr, cs, cr):
    x, y, z, c = place()
    plane, column = plane_peers(x, y, z, c), column_peers(x, y, z, c)
    partner = device(x, y, z, 1 - c)
    greet([t for _, t in plane] + [t for _, t in column] + [partner])
    out_ref[z, y, c, x, 0:4, :] = att_ref[:, 0:128]
    out_ref[z, y, c, x, 4:8, :] = att_ref[:, 128:256]
    mine = out_ref.at[z, y, c, x]
    first = [remote(mine, mine, zs.at[i], zr.at[i], t) for i, (_, t) in enumerate(column)]
    for copy in first:
        copy.start()
    for copy in first:
        copy.wait_recv()
    mine = out_ref.at[:, y, c, x]
    second = [remote(mine, mine, ps.at[i], pr.at[i], t) for i, (_, t) in enumerate(plane)]
    for copy in second:
        copy.start()
    for copy in second:
        copy.wait_recv()
    mine = out_ref.at[:, :, c]
    third = remote(mine, mine, cs, cr, partner)
    third.start()
    for copy in first + second:
        copy.wait_send()
    third.wait()


def split(value):
    high = value.astype(bf16)
    low = (value - high.astype(f32)).astype(bf16)
    return high, low


def cholesky(entries, size):
    lower = [[None] * size for _ in range(size)]
    inverse = [None] * size
    for col in range(size):
        total = entries(col, col)
        for k in range(col):
            total = total - lower[col][k] * lower[col][k]
        inverse[col] = 1.0 / jnp.sqrt(total)
        for row in range(col + 1, size):
            acc = entries(row, col)
            for k in range(col):
                acc = acc - lower[row][k] * lower[col][k]
            lower[row][col] = acc * inverse[col]
    return lower, inverse


def substitute(lower, inverse, rhs, size):
    forward = []
    for row in range(size):
        acc = rhs[row]
        for k in range(row):
            acc = acc - lower[row][k] * forward[k]
        forward.append(acc * inverse[row])
    answer = [None] * size
    for row in reversed(range(size)):
        acc = forward[row]
        for k in range(row + 1, size):
            acc = acc - lower[k][row] * answer[k]
        answer[row] = acc * inverse[row]
    return answer


def crossing_kernel(
    counts, owners, slots, att, star, axis, observed, phase, offset,
    step_ref, pay, basis, cross, pairs, table, first, offs, sums, used, where_to,
):
    def clear(i, carry):
        pay[pl.ds(i * 64, 64), :] = jnp.zeros((64, 128), f32)
        return carry

    lax.fori_loop(0, 11 * DEV // 64, clear, 0)

    def clear_used(i, carry):
        used[i] = 0
        return carry

    lax.fori_loop(0, DEV, clear_used, 0)
    for pad in (5, 6, 7, 13, 14, 15):
        pairs[pad * TR:(pad + 1) * TR, :] = jnp.zeros((TR, 128), f32)
    sub8 = lax.broadcasted_iota(jnp.int32, (8, 128), 0)
    lane8 = lax.broadcasted_iota(jnp.int32, (8, 128), 1)

    for c in range(CELLS_HERE):
        lanes = slice(c * CS, (c + 1) * CS)

        def prepare(g, acc, c=c, lanes=lanes):
            rows = pl.ds(pl.multiple_of(g * 8, 8), 8)
            here = c * NT + g * 8
            live = jnp.where(sub8 + g * 8 < counts[c], 1.0, 0.0)
            t = phase[rows, lanes]
            square = t * t
            cube = square * t
            rest = 1.0 - t
            b = [
                rest * rest * rest * (1.0 / 6.0) * live,
                (3.0 * cube - 6.0 * square + 4.0) * (1.0 / 6.0) * live,
                (-3.0 * cube + 3.0 * square + 3.0 * t + 1.0) * (1.0 / 6.0) * live,
                cube * (1.0 / 6.0) * live,
            ]
            offs[pl.ds(pl.multiple_of(here, 8), 8), :] = offset[rows, lanes]
            for i in range(4):
                basis[pl.ds(pl.multiple_of(i * TR + here, 8), 8), :] = b[i]
            for n, (shift, i) in enumerate(SHIFTS):
                cross[pl.ds(pl.multiple_of(n * TR + here, 8), 8), :] = b[i] * b[i + shift]
            a = [axis[m, rows, lanes] for m in range(4)]
            for n, (i, j) in enumerate(PAIRS):
                pairs[pl.ds(pl.multiple_of(PAIR_ROW[n] * TR + here, 8), 8), :] = a[i] * a[j]
            p = [star[m, rows, lanes] * live for m in range(5)]
            terms = [p[i] * p[j] for i in range(5) for j in range(i + 1)]
            return tuple(s + term for s, term in zip(acc, terms))

        acc = lax.fori_loop(0, NT // 8, prepare, tuple(jnp.zeros((8, 128), f32) for _ in range(15)))
        for n in range(15):
            sums[n:n + 1, lanes] = jnp.sum(acc[n], axis=0, keepdims=True)

    knot = lax.broadcasted_iota(jnp.int32, (16, 128), 0)

    def spread(rows, hits, count):
        value = jnp.zeros((16, 128), f32)
        for i in reversed(range(count)):
            value = jnp.where(hits[i], jnp.broadcast_to(rows[i], (16, 128)), value)
        return value

    def hits_of(at):
        row = offs[pl.ds(at, 1), :]
        gap = knot - jnp.broadcast_to(row, (16, 128))
        return [gap == i for i in range(4)]

    def normals(g, carry):
        c, base = g // 8, (g % 8) * 8
        for jj in range(8):
            j = base + jj
            at = g * 8 + jj
            hits = hits_of(at)
            parts = []
            for shift in range(4):
                rows = [cross[pl.ds(SHIFT_OF[(shift, i)] * TR + at, 1), :] for i in range(4 - shift)]
                parts.append(spread(rows, hits, 4 - shift))
            right = jnp.concatenate(parts, axis=0)
            left = pairs[pl.ds(at, 16, stride=TR), :]
            rh, rl = split(right)
            lh, ll = split(left)
            out = lax.dot_general(
                jnp.concatenate([lh, ll], axis=0), jnp.concatenate([rh, rl], axis=0),
                (((1,), (1,)), ((), ())), preferred_element_type=f32,
            )
            total = out[0:16] + out[16:32]
            total = total + pltpu.roll(total, 64, 1)
            packed = jnp.where(lane8 < 64, total[0:8], total[8:16])
            owner, slot = owners[c, j], slots[c, j]
            rank = used[owner]
            used[owner] = rank + 1
            ox, oc, oy, oz = owner % 4, (owner // 4) % 2, (owner // 8) % 4, owner // 32
            q = (ox * NY + oy) * QIN + oc * NZ + oz
            where_to[at] = q + rank * DEV
            packed = jnp.where((sub8 == 0) & (lane8 == ID_LANE), slot.astype(f32), packed)
            pay[pl.ds(rank * 5 * DEV + q, 5, stride=DEV), :] = packed[0:5]
            rows4 = att[pl.ds(owner * 8 + (slot // 8) * 4, 4), :]
            table[pl.ds(at, 4, stride=TR), :] = pltpu.roll(rows4, (128 - (slot % 8) * 16) % 128, 1)
        return carry

    lax.fori_loop(0, TR // 8, normals, 0)

    for c in range(CELLS_HERE):
        lanes = slice(c * CS, (c + 1) * CS)

        def predict(g, acc, c=c, lanes=lanes):
            rows = pl.ds(pl.multiple_of(g * 8, 8), 8)
            here = c * NT + g * 8
            live = jnp.where(sub8 + g * 8 < counts[c], 1.0, 0.0)
            off = offset[rows, lanes]
            value = live * observed[rows, lanes]
            b = [basis[pl.ds(pl.multiple_of(i * TR + here, 8), 8), :] for i in range(4)]
            for m in range(4):
                tab = table[pl.ds(pl.multiple_of(m * TR + here, 8), 8), :]
                fit = b[0] * jnp.take_along_axis(tab, off, axis=1)
                for i in range(1, 4):
                    fit = fit + b[i] * jnp.take_along_axis(tab, off + i, axis=1)
                value = value - axis[m, rows, lanes] * fit
            first[pl.ds(pl.multiple_of(here, 8), 8), :] = value
            return tuple(s + star[n, rows, lanes] * value for n, s in enumerate(acc))

        acc = lax.fori_loop(0, NT // 8, predict, tuple(jnp.zeros((8, 128), f32) for _ in range(5)))
        for n in range(5):
            sums[15 + n:16 + n, lanes] = jnp.sum(acc[n], axis=0, keepdims=True)

    def entry(i, j):
        n = i * (i + 1) // 2 + j
        return sums[n:n + 1, :] + (1.0 if i == j else 0.0)

    lower, inverse = cholesky(entry, 5)
    steps = substitute(lower, inverse, [sums[15 + n:16 + n, :] for n in range(5)], 5)
    for n in range(5):
        step_ref[n:n + 1, :] = steps[n]

    lane32 = lax.broadcasted_iota(jnp.int32, (32, 128), 1)
    row32 = lax.broadcasted_iota(jnp.int32, (32, 128), 0)
    own = (lane32 // 16) == (row32 % 8)
    lane1 = lax.broadcasted_iota(jnp.int32, (1, 128), 1)

    def gradients(g, carry):
        c, base = g // 8, pl.multiple_of((g % 8) * 8, 8)
        rows = pl.ds(base, 8)
        lanes = pl.ds(pl.multiple_of(c * CS, CS), CS)
        at = pl.multiple_of(g * 8, 8)
        live = jnp.where(sub8 + base < counts[c], 1.0, 0.0)
        fitted = star[0, rows, lanes] * step_ref[0:1, lanes]
        for n in range(1, 5):
            fitted = fitted + star[n, rows, lanes] * step_ref[n:n + 1, lanes]
        second = first[pl.ds(at, 8), :] - live * fitted
        left = jnp.concatenate([axis[m, rows, lanes] * second for m in range(4)], axis=0)
        parts = []
        for jj in range(8):
            hits = hits_of(at + jj)
            parts.append(spread([basis[pl.ds(i * TR + at + jj, 1), :] for i in range(4)], hits, 4))
        lh, ll = split(left)
        rh, rl = split(jnp.concatenate(parts, axis=0))
        out = lax.dot_general(
            jnp.concatenate([lh, ll], axis=0), jnp.concatenate([rh, rl], axis=0),
            (((1,), (1,)), ((), ())), preferred_element_type=f32,
        )
        total = out[0:32, 0:128] + out[0:32, 128:256] + out[32:64, 0:128]
        total = jnp.where(own, total, 0.0)
        for shift in (64, 32, 16):
            total = total + pltpu.roll(total, shift, 1)
        grad = jnp.zeros((8, 128), f32)
        for m in range(4):
            grad = jnp.where((lane8 // 16) % 4 == m, total[m * 8:(m + 1) * 8], grad)
        for jj in range(8):
            code = where_to[at + jj]
            q, rank = code % DEV, code // DEV
            old = pay[pl.ds(10 * DEV + q, 1), :]
            pay[pl.ds(10 * DEV + q, 1), :] = jnp.where(lane1 // 64 == rank, grad[jj:jj + 1], old)
        return carry

    lax.fori_loop(0, TR // 8, gradients, 0)


def exchange_kernel(pay, out, got, comb, part, zsum, zgot, ps, pr, cs, cr, zs, zr, hs, hr):
    x, y, z, c = place()
    plane, column = plane_peers(x, y, z, c), column_peers(x, y, z, c)
    partner = device(x, y, z, 1 - c)
    rank = ((z * NY + y) * NC + c) * NX + x
    after, before = (rank + 1) % DEV, (rank + DEV - 1) % DEV
    right, left = (after // NX, after % NX), (before // NX, before % NX)
    greet([t for _, t in plane] + [t for _, t in column] + [partner, right, left])
    here = x * NY + y
    copies = [
        remote(pay.at[:, pl.ds(p * QIN, QIN), :], got.at[here], ps.at[i], pr.at[i], t)
        for i, (p, t) in enumerate(plane)
    ]
    for copy in copies:
        copy.start()
    got[here] = pay[:, pl.ds(pl.multiple_of(here * QIN, QIN), QIN), :]
    for copy in copies:
        copy.wait_recv()

    rows = NP * QIN
    cols = QIN * KB
    row = lax.broadcasted_iota(jnp.int32, (rows, cols), 0)
    col = lax.broadcasted_iota(jnp.int32, (rows, cols), 1)
    local = (col - (row % QIN) * KB).astype(f32)
    picks = []
    for s in range(2):
        ids = got[:, s * 5, :, :].reshape(rows, 128)[:, ID_LANE:ID_LANE + 1]
        picks.append(jnp.where(local == ids, 1.0, 0.0).T)
    pick = jnp.concatenate(picks, axis=1).astype(bf16)
    lane = lax.broadcasted_iota(jnp.int32, (rows, 128), 1)
    for r in range(6):
        if r < 5:
            data = jnp.concatenate([got[:, s * 5 + r, :, :].reshape(rows, 128) for s in range(2)], axis=0)
        else:
            both = got[:, 10, :, :].reshape(rows, 128)
            data = jnp.concatenate([jnp.where(lane < 64, both, 0.0), jnp.where(lane < 64, 0.0, both)], axis=0)
        high, low = split(data)
        comb[r] = jnp.dot(pick, high, preferred_element_type=f32) + jnp.dot(pick, low, preferred_element_type=f32)

    half = NZ * KB
    swap = remote(comb.at[:, pl.ds(pl.multiple_of((1 - c) * half, half), half), :], part, cs, cr, partner)
    swap.start()
    swap.wait_recv()
    zsum[...] = comb[:, pl.ds(pl.multiple_of(c * half, half), half), :] + part[...]
    along = [
        remote(zsum.at[:, pl.ds(zz * KB, KB), :], zgot.at[z], zs.at[i], zr.at[i], t)
        for i, (zz, t) in enumerate(column)
    ]
    for copy in along:
        copy.start()
    zgot[z] = zsum[:, pl.ds(pl.multiple_of(z * KB, KB), KB), :]
    for copy in along:
        copy.wait_recv()
    total = zgot[0]
    for i in range(1, NZ):
        total = total + zgot[i]
    out[:, 8:24, :] = total
    halo = [
        remote(out.at[:, 16:24, :], out.at[:, 0:8, :], hs.at[0], hr.at[0], right),
        remote(out.at[:, 8:16, :], out.at[:, 24:32, :], hs.at[1], hr.at[1], left),
    ]
    for copy in halo:
        copy.start()
    for copy in copies + [swap] + along:
        copy.wait_send()
    for copy in halo:
        copy.wait()


def sweep_kernel(red, out):
    rank = lax.axis_index("cells") * NX + lax.axis_index("tm")
    shape = (32, 128)
    row = lax.broadcasted_iota(jnp.int32, shape, 0)
    lane = lax.broadcasted_iota(jnp.int32, shape, 1)
    k = lane % KB
    beyond = ((row == 7) & (rank == 0)) | ((row == 24) & (rank == DEV - 1))
    valid = jnp.where(beyond, 0.0, 1.0)
    ahead, behind = {}, {}
    for n in range(10):
        comp = red[n % 5]
        start = (n // 5) * 64
        for t in range(4):
            value = jnp.take_along_axis(comp, start + t * 16 + k, axis=1)
            ahead[n, t] = jnp.where(k + t < KB, value, 0.0) if t else value
            if t:
                value = jnp.take_along_axis(comp, start + t * 16 + (k + KB - t) % KB, axis=1)
                behind[n, t] = jnp.where(k >= t, value, 0.0)
    for n, (i, j) in enumerate(PAIRS):
        if i == j:
            ahead[n, 0] = ahead[n, 0] + 34.0
    fold = red[5]
    fold = fold + pltpu.roll(fold, 64, 1)
    gradient = [jnp.take_along_axis(fold, m * KB + k, axis=1) for m in range(4)]

    def pair(i, j):
        return PAIR_OF[(min(i, j), max(i, j))]

    lower, inverse = cholesky(lambda i, j: ahead[pair(i, j), 0], 4)
    x = [0.5 * v * valid for v in substitute(lower, inverse, gradient, 4)]
    for _ in range(ITERS - 1):
        misfit = list(gradient)
        for n in range(4):
            up = {t: pltpu.roll(x[n], 128 - t, 1) for t in (1, 2, 3)}
            down = {t: pltpu.roll(x[n], t, 1) for t in (1, 2, 3)}
            for m in range(4):
                p = pair(m, n)
                acc = ahead[p, 0] * x[n]
                for t in (1, 2, 3):
                    acc = acc + ahead[p, t] * up[t] + behind[p, t] * down[t]
                misfit[m] = misfit[m] - acc
            before = jnp.where(k == 0, pltpu.roll(down[1], 1, 0), down[1])
            after = jnp.where(k == KB - 1, pltpu.roll(up[1], 31, 0), up[1])
            misfit[n] = misfit[n] + 16.0 * (before + after)
        x = [(v + 0.5 * w) * valid for v, w in zip(x, substitute(lower, inverse, misfit, 4))]
    sub8 = lax.broadcasted_iota(jnp.int32, (8, 128), 0)
    keep = sub8 == lax.broadcasted_iota(jnp.int32, (8, 128), 1) // KB
    for m in range(4):
        for h in range(2):
            part = jnp.where(keep, x[m][8 + h * 8:16 + h * 8], 0.0)
            out[m:m + 1, h * 128:(h + 1) * 128] = jnp.sum(part, axis=0, keepdims=True)


def per_device(
    attitude, star_partials, attitude_partials, observed, phase, knot_offset, cell_counts, interval_owner, block_slot
):
    dma = pltpu.SemaphoreType.DMA
    whole = pl.pallas_call(
        gather_kernel,
        out_shape=jax.ShapeDtypeStruct((NZ, NY, NC, NX, 8, 128), f32),
        in_specs=[VMEM],
        out_specs=VMEM,
        scratch_shapes=[dma((NZ - 1,)), dma((NZ - 1,)), dma((NP - 1,)), dma((NP - 1,)), dma, dma],
        compiler_params=pltpu.CompilerParams(collective_id=0, has_side_effects=True),
        name="gather_attitude",
    )(attitude)
    star_step, pay = pl.pallas_call(
        crossing_kernel,
        out_shape=(
            jax.ShapeDtypeStruct((5, CELLS_HERE * CS), f32),
            jax.ShapeDtypeStruct((11 * DEV, 128), f32),
        ),
        in_specs=[SMEM, SMEM, SMEM] + [VMEM] * 6,
        out_specs=(VMEM, VMEM),
        scratch_shapes=[
            pltpu.VMEM((4 * TR, 128), f32),
            pltpu.VMEM((10 * TR, 128), f32),
            pltpu.VMEM((16 * TR, 128), f32),
            pltpu.VMEM((4 * TR, 128), f32),
            pltpu.VMEM((TR, 128), f32),
            pltpu.VMEM((TR, 128), jnp.int32),
            pltpu.VMEM((24, CELLS_HERE * CS), f32),
            pltpu.SMEM((DEV,), jnp.int32),
            pltpu.SMEM((TR,), jnp.int32),
        ],
        name="crossings",
    )(
        cell_counts, interval_owner.reshape(CELLS_HERE, NT), block_slot, whole.reshape(DEV * 8, 128),
        star_partials, attitude_partials, observed, phase, knot_offset,
    )
    reduced = pl.pallas_call(
        exchange_kernel,
        out_shape=jax.ShapeDtypeStruct((6, 32, 128), f32),
        in_specs=[VMEM],
        out_specs=VMEM,
        scratch_shapes=[
            pltpu.VMEM((NP, 11, QIN, 128), f32),
            pltpu.VMEM((6, QIN * KB, 128), f32),
            pltpu.VMEM((6, NZ * KB, 128), f32),
            pltpu.VMEM((6, NZ * KB, 128), f32),
            pltpu.VMEM((NZ, 6, KB, 128), f32),
            dma((NP - 1,)), dma((NP - 1,)), dma, dma, dma((NZ - 1,)), dma((NZ - 1,)), dma((2,)), dma((2,)),
        ],
        compiler_params=pltpu.CompilerParams(collective_id=1, has_side_effects=True),
        name="exchange",
    )(pay.reshape(11, DEV, 128))
    attitude_step = pl.pallas_call(
        sweep_kernel,
        out_shape=jax.ShapeDtypeStruct((4, 256), f32),
        in_specs=[VMEM],
        out_specs=VMEM,
        name="sweeps",
    )(reduced)
    return (star_step, attitude_step)


def solution(mesh):
    both = ("cells", "tm")
    placed = (
        P(None, both), P(None, None, both), P(None, None, both), P(None, both), P(None, both), P(None, both),
        P(both), P(both, None, None), P(both, None),
    )
    return jax.shard_map(
        per_device, mesh=mesh, in_specs=placed, out_specs=(P(None, both), P(None, both)), check_vma=False
    )
```

time: 751 us -> 114 us (0.15)
  the two profiles are of different devices: /device:TPU:127 before, /device:TPU:26 now
where the time goes in v1:
time: 114 us
  Pallas kernels  113 us (99%)
    pallas_call x1, Pallas kernels, per_device(): pl.pallas_call(exchange_kernel, out_shape=jax.ShapeDtypeStruct((6, 32, 12...  51.3 us
    pallas_call x1, Pallas kernels, per_device(): pl.pallas_call(crossing_kernel, out_shape=(jax.ShapeDtypeStruct((5, CELLS...  34.5 us
    pallas_call x1, Pallas kernels, per_device(): pl.pallas_call(gather_kernel, out_shape=jax.ShapeDtypeStruct((NZ, NY, NC,...  24 us
    pallas_call x1, Pallas kernels, per_device(): pl.pallas_call(sweep_kernel, out_shape=jax.ShapeDtypeStruct((4, 256), f32...  3.35 us

profile of v1, /device:TPU:26, one launch (start us, length us, event | category | flops | bytes accessed | tf_op | source)
XLA Modules:
  0.0 113.8 jit_solution(4940672428732221820)
XLA Ops:
  0.6 24.0 %gather_attitude.1 = f32[8,4,2,4,8,128]{5,4,3,2,1,0:T(8,128)} custom-call(f32[4,256]{1,0:T(4,128)} %att_ref.1), custom_call_target="tpu_custom_call" | custom-call | tf_op jit(solution)/shard_map/gather_attitude/pallas_call | solution.py:432
  24.6 34.5 %crossings.1 = (f32[5,512]{1,0:T(8,128)}, f32[2816,128]{1,0:T(8,128)}) custom-call(s32[4]{0:T(128)} %counts.1, s32[4,64]{1,0:T(4,128)} %bitcast.5, s32[4,64]{1,0:T(4,128)} %slots.1, f32[2048,128]{1,0:T(8,128)} %bitcast.3, f32[5,64,512]{2,1,0:T(8,128)} %star.1, f32[4,64,512]{2,1,0:T(8,128)} %axis.1, f32[64,512]{1,0:T(8,128)} %observed.1, f32[64,512]{1,0:T(8,128)} %phase.1, ...), custom_call_target="tpu_custom_call" | custom-call | tf_op jit(solution)/shard_map/crossings/pallas_call | solution.py:441
  59.2 51.3 %exchange.1.red = f32[6,32,128]{2,1,0:T(8,128)} custom-call(f32[11,256,128]{2,1,0:T(8,128)} %bitcast.4), custom_call_target="tpu_custom_call" | custom-call | tf_op jit(solution)/shard_map/exchange/pallas_call | solution.py:465
  110.5 3.4 %sweeps.1 = f32[4,256]{1,0:T(4,128)} custom-call(f32[6,32,128]{2,1,0:T(8,128)} %exchange.1.red), custom_call_target="tpu_custom_call" | custom-call | tf_op jit(solution)/shard_map/sweeps/pallas_call | solution.py:481

commit v2 on v1

v2 whole, which is shorter than its diff:
```python
import functools

import jax
import jax.numpy as jnp
from jax import lax
from jax.experimental import pallas as pl
from jax.experimental.pallas import tpu as pltpu
from jax.sharding import PartitionSpec as P

NT, CS, KB, ITERS = 64, 128, 16, 6
NX, NY, NZ, NC = 4, 4, 8, 2
NP = NX * NY
DEV = NP * NZ * NC
QIN = NZ * NC
CELLS_HERE = 4
TR = CELLS_HERE * NT
ID_LANE = 63
MESH = pl.DeviceIdType.MESH
f32, bf16 = jnp.float32, jnp.bfloat16
PAIRS = [(m, n) for m in range(4) for n in range(m, 4)]
PAIR_OF = {pair: i for i, pair in enumerate(PAIRS)}
SHIFTS = [(t, i) for t in range(4) for i in range(4 - t)]
SHIFT_OF = {pair: i for i, pair in enumerate(SHIFTS)}
VMEM = pl.BlockSpec(memory_space=pltpu.VMEM)
SMEM = pl.BlockSpec(memory_space=pltpu.SMEM)


def place():
    cells, x = lax.axis_index("cells"), lax.axis_index("tm")
    z, y, c = cells // (NY * NC), (cells // NC) % NY, cells % NC
    return x, y, z, c


def device(x, y, z, c):
    return ((z * NY + y) * NC + c, x)


def remote(src, dst, send, recv, target):
    return pltpu.make_async_remote_copy(
        src_ref=src, dst_ref=dst, send_sem=send, recv_sem=recv, device_id=target, device_id_type=MESH
    )


def plane_peers(x, y, z, c):
    here = x * NY + y
    peers = []
    for i in range(1, NP):
        there = (here + i) % NP
        peers.append((there, device(there // NY, there % NY, z, c)))
    return peers


def column_peers(x, y, z, c):
    return [((z + i) % NZ, device(x, y, (z + i) % NZ, c)) for i in range(1, NZ)]


def greet(targets):
    barrier = pltpu.get_barrier_semaphore()
    for target in targets:
        pl.semaphore_signal(barrier, inc=1, device_id=target, device_id_type=MESH)
    pl.semaphore_wait(barrier, len(targets))


def split(value):
    high = value.astype(bf16)
    low = (value - high.astype(f32)).astype(bf16)
    return high, low


def cholesky(entries, size):
    lower = [[None] * size for _ in range(size)]
    inverse = [None] * size
    for col in range(size):
        total = entries(col, col)
        for k in range(col):
            total = total - lower[col][k] * lower[col][k]
        inverse[col] = 1.0 / jnp.sqrt(total)
        for row in range(col + 1, size):
            acc = entries(row, col)
            for k in range(col):
                acc = acc - lower[row][k] * lower[col][k]
            lower[row][col] = acc * inverse[col]
    return lower, inverse


def substitute(lower, inverse, rhs, size):
    forward = []
    for row in range(size):
        acc = rhs[row]
        for k in range(row):
            acc = acc - lower[row][k] * forward[k]
        forward.append(acc * inverse[row])
    answer = [None] * size
    for row in reversed(range(size)):
        acc = forward[row]
        for k in range(row + 1, size):
            acc = acc - lower[k][row] * answer[k]
        answer[row] = acc * inverse[row]
    return answer


def spline(t, live):
    square = t * t
    cube = square * t
    rest = 1.0 - t
    return [
        rest * rest * rest * (1.0 / 6.0) * live,
        (3.0 * cube - 6.0 * square + 4.0) * (1.0 / 6.0) * live,
        (-3.0 * cube + 3.0 * square + 3.0 * t + 1.0) * (1.0 / 6.0) * live,
        cube * (1.0 / 6.0) * live,
    ]


def spread(rows, hits):
    value = jnp.zeros((16, 128), f32)
    for row, hit in reversed(list(zip(rows, hits))):
        value = jnp.where(hit, jnp.broadcast_to(row, (16, 128)), value)
    return value


def nt_dot(left, right):
    return lax.dot_general(left, right, (((1,), (1,)), ((), ())), preferred_element_type=f32)


def aligned(value):
    return pl.multiple_of(value, 8)


def normal_kernel(counts, owners, slots, axis, phase, offset, pay, codes, cross, parts, offs, used):
    sub8 = lax.broadcasted_iota(jnp.int32, (8, 128), 0)
    lane8 = lax.broadcasted_iota(jnp.int32, (8, 128), 1)

    def clear(i, carry):
        pay[pl.ds(aligned(i * 128), 128), :] = jnp.zeros((128, 128), f32)
        return carry

    lax.fori_loop(0, 10 * DEV // 128, clear, 0)
    for c in range(CELLS_HERE):
        lanes = slice(c * CS, (c + 1) * CS)

        def prepare(g, carry, c=c, lanes=lanes):
            rows = pl.ds(aligned(g * 8), 8)
            here = c * NT + g * 8
            live = jnp.where(sub8 + g * 8 < counts[c], 1.0, 0.0)
            b = spline(phase[rows, lanes], live)
            offs[pl.ds(aligned(here), 8), :] = offset[rows, lanes]
            for n, (shift, i) in enumerate(SHIFTS):
                cross[pl.ds(aligned(n * TR + here), 8), :] = b[i] * b[i + shift]
            for m in range(4):
                parts[pl.ds(aligned(m * TR + here), 8), :] = axis[m, rows, lanes]
            for i in range(8):
                used[here + i] = 0
            return carry

        lax.fori_loop(0, NT // 8, prepare, 0)

    knot = lax.broadcasted_iota(jnp.int32, (16, 128), 0)

    def normals(g, carry):
        c, base = lax.shift_right_logical(g, 3), (g & 7) * 8
        for jj in range(8):
            at = g * 8 + jj
            gap = knot - jnp.broadcast_to(offs[pl.ds(at, 1), :], (16, 128))
            hits = [gap == i for i in range(4)]
            right = jnp.concatenate(
                [
                    spread([cross[pl.ds(SHIFT_OF[(s, i)] * TR + at, 1), :] for i in range(4 - s)], hits)
                    for s in range(4)
                ],
                axis=0,
            )
            a = [jnp.broadcast_to(parts[pl.ds(m * TR + at, 1), :], (8, 128)) for m in range(4)]
            top = jnp.where(sub8 == 4, a[1], a[0]) * jnp.where(
                sub8 == 0, a[0], jnp.where(sub8 == 2, a[2], jnp.where(sub8 == 3, a[3], a[1]))
            )
            bottom = jnp.where(sub8 < 2, a[1], jnp.where(sub8 == 4, a[3], a[2])) * jnp.where(
                (sub8 == 0) | (sub8 == 2), a[2], a[3]
            )
            rh, rl = split(right)
            lh, ll = split(jnp.concatenate([top, bottom], axis=0))
            out = nt_dot(jnp.concatenate([lh, ll], axis=0), jnp.concatenate([rh, rl], axis=0))
            total = out[0:16] + out[16:32]
            total = total + pltpu.roll(total, 64, 1)
            packed = jnp.where(lane8 < 64, total[0:8], total[8:16])
            owner, slot = owners[c, base + jj], slots[c, base + jj]
            rank = used[owner]
            used[owner] = rank + 1
            plane = ((owner & 3) << 2) | ((owner >> 3) & 3)
            q = (plane << 4) | ((owner & 4) << 1) | (owner >> 5)
            packed = jnp.where((sub8 == 0) & (lane8 == ID_LANE), slot.astype(f32), packed)
            pay[pl.ds(rank * (5 * DEV) + q, 5, stride=DEV), :] = packed[0:5]
            codes[pl.ds(at, 1), :] = jnp.full((1, 128), rank * DEV + q, jnp.int32)
        return carry

    lax.fori_loop(0, TR // 8, normals, 0)


def main_kernel(
    counts, owners, slots, att_in, pay, codes, star, axis, observed, phase, offset,
    step_ref, out,
    att, sh, sl, tile, otile, table, first, sums, order, grads, gpay, got, ggot, comb, part, zsum, zgot,
    zs, zr, ps, pr, cs, cr, ns, nr, gs, gr, ws, wr, us, ur, vs, vr, hs, hr,
):
    x, y, z, c = place()
    plane, column = plane_peers(x, y, z, c), column_peers(x, y, z, c)
    partner = device(x, y, z, 1 - c)
    rank = ((z * NY + y) * NC + c) * NX + x
    after, before = (rank + 1) % DEV, (rank + DEV - 1) % DEV
    right, left = (after // NX, after % NX), (before // NX, before % NX)
    greet([t for _, t in plane] + [t for _, t in column] + [partner, right, left])
    here = x * NY + y
    sent = []

    att[z, y, c, x, 0:4, :] = att_in[:, 0:128]
    att[z, y, c, x, 4:8, :] = att_in[:, 128:256]
    mine = att.at[z, y, c, x]
    gather_z = [remote(mine, mine, zs.at[i], zr.at[i], t) for i, (_, t) in enumerate(column)]
    for copy in gather_z:
        copy.start()

    sub8 = lax.broadcasted_iota(jnp.int32, (8, 128), 0)
    lane8 = lax.broadcasted_iota(jnp.int32, (8, 128), 1)
    knot = lax.broadcasted_iota(jnp.int32, (16, 128), 0)

    def spreads(cell):
        lanes = slice(cell * CS, (cell + 1) * CS)

        def body(g, acc):
            rows = pl.ds(aligned(g * 8), 8)
            live = jnp.where(sub8 + g * 8 < counts[cell], 1.0, 0.0)
            b = spline(phase[rows, lanes], live)
            otile[...] = offset[rows, lanes]
            for i in range(4):
                tile[i * 8:(i + 1) * 8, :] = b[i]
            pieces = []
            for jj in range(8):
                gap = knot - jnp.broadcast_to(otile[jj:jj + 1, :], (16, 128))
                pieces.append(spread([tile[i * 8 + jj:i * 8 + jj + 1, :] for i in range(4)], [gap == i for i in range(4)]))
            high, low = split(jnp.concatenate(pieces, axis=0))
            where = pl.ds(pl.multiple_of((cell * 8 + g) * 128, 128), 128)
            sh[where, :] = high
            sl[where, :] = low
            p = [star[m, rows, lanes] * live for m in range(5)]
            terms = [p[i] * p[j] for i in range(5) for j in range(i + 1)]
            return tuple(s + term for s, term in zip(acc, terms))

        acc = lax.fori_loop(0, NT // 8, body, tuple(jnp.zeros((8, 128), f32) for _ in range(15)))
        for n in range(15):
            sums[n:n + 1, lanes] = jnp.sum(acc[n], axis=0, keepdims=True)

    spreads(0)
    spreads(1)

    for copy in gather_z:
        copy.wait_recv()
    mine = att.at[:, y, c, x]
    gather_p = [remote(mine, mine, ps.at[i], pr.at[i], t) for i, (_, t) in enumerate(plane)]
    for copy in gather_p:
        copy.start()
    terms = [
        remote(pay.at[:, pl.ds(p * QIN, QIN), :], got.at[here], ns.at[i], nr.at[i], t)
        for i, (p, t) in enumerate(plane)
    ]
    for copy in terms:
        copy.start()
    got[here] = pay[:, pl.ds(pl.multiple_of(here * QIN, QIN), QIN), :]

    spreads(2)
    spreads(3)

    def entry(i, j):
        n = i * (i + 1) // 2 + j
        return sums[n:n + 1, :] + (1.0 if i == j else 0.0)

    lower, inverse = cholesky(entry, 5)
    target = lax.broadcasted_iota(jnp.int32, (TR, DEV), 1)
    code = jnp.broadcast_to(codes[:, 0:1], (TR, DEV))
    for s in range(2):
        order[:, s * TR:(s + 1) * TR] = jnp.where(code == target + s * DEV, 1.0, 0.0).T.astype(bf16)

    for copy in gather_p:
        copy.wait_recv()
    mine = att.at[:, :, c]
    gather_c = remote(mine, mine, cs, cr, partner)
    gather_c.start()
    gather_c.wait_recv()

    lane4 = lax.broadcasted_iota(jnp.int32, (4, 128), 1) // KB

    def choose(g, carry):
        cell, base = lax.shift_right_logical(g, 3), (g & 7) * 8
        for jj in range(8):
            owner, slot = owners[cell, base + jj], slots[cell, base + jj]
            rows4 = att[owner >> 5, (owner >> 3) & 3, (owner >> 2) & 1, owner & 3, pl.ds((slot >> 3) * 4, 4), :]
            table[pl.ds(g * 32 + jj, 4, stride=8), :] = jnp.where(lane4 == (slot & 7), rows4, 0.0)
        return carry

    lax.fori_loop(0, TR // 8, choose, 0)

    lane32 = lax.broadcasted_iota(jnp.int32, (32, 128), 1)
    row32 = lax.broadcasted_iota(jnp.int32, (32, 128), 0)
    own = (lane32 // KB) == (row32 % 8)

    def fold(value):
        for shift in (64, 32, 16):
            value = value + pltpu.roll(value, shift, 1)
        return value

    for cell in range(CELLS_HERE):
        lanes = slice(cell * CS, (cell + 1) * CS)

        def predict(g, acc, cell=cell, lanes=lanes):
            rows = pl.ds(aligned(g * 8), 8)
            gg = cell * 8 + g
            live = jnp.where(sub8 + g * 8 < counts[cell], 1.0, 0.0)
            coeff = jnp.where(own, fold(table[pl.ds(aligned(gg * 32), 32), :]), 0.0)
            high, low = split(coeff)
            where = pl.ds(pl.multiple_of(gg * 128, 128), 128)
            big = jnp.dot(jnp.concatenate([high, low], axis=0), sh[where, :], preferred_element_type=f32)
            fit = big[0:32] + big[32:64] + jnp.dot(high, sl[where, :], preferred_element_type=f32)
            value = live * observed[rows, lanes]
            for m in range(4):
                value = value - axis[m, rows, lanes] * fit[m * 8:(m + 1) * 8]
            first[pl.ds(aligned(gg * 8), 8), :] = value
            return tuple(s + star[n, rows, lanes] * value for n, s in enumerate(acc))

        acc = lax.fori_loop(0, NT // 8, predict, tuple(jnp.zeros((8, 128), f32) for _ in range(5)))
        for n in range(5):
            sums[15 + n:16 + n, lanes] = jnp.sum(acc[n], axis=0, keepdims=True)

    steps = substitute(lower, inverse, [sums[15 + n:16 + n, :] for n in range(5)], 5)
    for n in range(5):
        step_ref[n:n + 1, :] = steps[n]

    for cell in range(CELLS_HERE):
        lanes = slice(cell * CS, (cell + 1) * CS)

        def gradients(g, carry, cell=cell, lanes=lanes):
            rows = pl.ds(aligned(g * 8), 8)
            gg = cell * 8 + g
            live = jnp.where(sub8 + g * 8 < counts[cell], 1.0, 0.0)
            fitted = star[0, rows, lanes] * step_ref[0:1, lanes]
            for n in range(1, 5):
                fitted = fitted + star[n, rows, lanes] * step_ref[n:n + 1, lanes]
            second = first[pl.ds(aligned(gg * 8), 8), :] - live * fitted
            high, low = split(jnp.concatenate([axis[m, rows, lanes] * second for m in range(4)], axis=0))
            where = pl.ds(pl.multiple_of(gg * 128, 128), 128)
            big = nt_dot(jnp.concatenate([high, low], axis=0), sh[where, :])
            total = big[0:32] + big[32:64] + nt_dot(high, sl[where, :])
            total = fold(jnp.where(own, total, 0.0))
            grad = jnp.zeros((8, 128), f32)
            for m in range(4):
                grad = jnp.where((lane8 // KB) % 4 == m, total[m * 8:(m + 1) * 8], grad)
            grads[pl.ds(aligned(gg * 8), 8), :] = grad
            return carry

        lax.fori_loop(0, NT // 8, gradients, 0)

    lane = lax.broadcasted_iota(jnp.int32, (TR, 128), 1)

    def halves(both):
        return split(jnp.concatenate([jnp.where(lane < 64, both, 0.0), jnp.where(lane < 64, 0.0, both)], axis=0))

    high, low = halves(grads[...])
    gpay[...] = jnp.dot(order[...], high, preferred_element_type=f32) + jnp.dot(
        order[...], low, preferred_element_type=f32
    )
    gterms = [
        remote(gpay.at[pl.ds(p * QIN, QIN), :], ggot.at[here], gs.at[i], gr.at[i], t) for i, (p, t) in enumerate(plane)
    ]
    for copy in gterms:
        copy.start()
    ggot[here] = gpay[pl.ds(pl.multiple_of(here * QIN, QIN), QIN), :]

    for copy in terms:
        copy.wait_recv()
    rows = NP * QIN
    cols = QIN * KB
    row = lax.broadcasted_iota(jnp.int32, (rows, cols), 0)
    col = lax.broadcasted_iota(jnp.int32, (rows, cols), 1)
    local = (col - (row % QIN) * KB).astype(f32)
    for s in range(2):
        ids = got[:, s * 5, :, :].reshape(rows, 128)[:, ID_LANE:ID_LANE + 1]
        order[:, s * rows:(s + 1) * rows] = jnp.where(local == ids, 1.0, 0.0).T.astype(bf16)
    half = NZ * KB
    keep = pl.ds(pl.multiple_of(c * half, half), half)
    give = pl.ds(pl.multiple_of((1 - c) * half, half), half)

    def combine(r, high, low):
        comb[r] = jnp.dot(order[...], high, preferred_element_type=f32) + jnp.dot(
            order[...], low, preferred_element_type=f32
        )

    for r in range(5):
        data = jnp.concatenate([got[:, s * 5 + r, :, :].reshape(rows, 128) for s in range(2)], axis=0)
        combine(r, *split(data))
    five = pl.ds(0, 5)
    swap = remote(comb.at[five, give, :], part.at[five], ws.at[0], wr.at[0], partner)
    swap.start()
    for copy in gterms:
        copy.wait_recv()
    combine(5, *halves(ggot[...].reshape(rows, 128)))
    gswap = remote(comb.at[5, give, :], part.at[5], ws.at[1], wr.at[1], partner)
    gswap.start()
    swap.wait_recv()
    zsum[0:5] = comb[0:5, keep, :] + part[0:5]
    along = [
        remote(zsum.at[five, pl.ds(zz * KB, KB), :], zgot.at[z, five], us.at[i], ur.at[i], t)
        for i, (zz, t) in enumerate(column)
    ]
    for copy in along:
        copy.start()
    gswap.wait_recv()
    zsum[5] = comb[5, keep, :] + part[5]
    galong = [
        remote(zsum.at[5, pl.ds(zz * KB, KB), :], zgot.at[z, 5], vs.at[i], vr.at[i], t)
        for i, (zz, t) in enumerate(column)
    ]
    for copy in galong:
        copy.start()
    zgot[z] = zsum[:, pl.ds(pl.multiple_of(z * KB, KB), KB), :]
    for copy in along + galong:
        copy.wait_recv()
    total = zgot[0]
    for i in range(1, NZ):
        total = total + zgot[i]
    out[:, 8:24, :] = total
    halo = [
        remote(out.at[:, 16:24, :], out.at[:, 0:8, :], hs.at[0], hr.at[0], right),
        remote(out.at[:, 8:16, :], out.at[:, 24:32, :], hs.at[1], hr.at[1], left),
    ]
    for copy in halo:
        copy.start()
    for copy in gather_z + gather_p + [gather_c] + terms + gterms + [swap, gswap] + along + galong:
        copy.wait_send()
    for copy in halo:
        copy.wait()


def sweep_kernel(red, steps, out, steps_out):
    steps_out[...] = steps[...]
    rank = lax.axis_index("cells") * NX + lax.axis_index("tm")
    shape = (32, 128)
    row = lax.broadcasted_iota(jnp.int32, shape, 0)
    lane = lax.broadcasted_iota(jnp.int32, shape, 1)
    k = lane % KB
    beyond = ((row == 7) & (rank == 0)) | ((row == 24) & (rank == DEV - 1))
    valid = jnp.where(beyond, 0.0, 1.0)
    ahead, behind = {}, {}
    for n in range(10):
        comp = red[n % 5]
        start = (n // 5) * 64
        for t in range(4):
            value = jnp.take_along_axis(comp, start + t * 16 + k, axis=1)
            ahead[n, t] = jnp.where(k + t < KB, value, 0.0) if t else value
            if t:
                value = jnp.take_along_axis(comp, start + t * 16 + (k + KB - t) % KB, axis=1)
                behind[n, t] = jnp.where(k >= t, value, 0.0)
    for n, (i, j) in enumerate(PAIRS):
        if i == j:
            ahead[n, 0] = ahead[n, 0] + 34.0
    fold = red[5]
    fold = fold + pltpu.roll(fold, 64, 1)
    gradient = [jnp.take_along_axis(fold, m * KB + k, axis=1) for m in range(4)]

    def pair(i, j):
        return PAIR_OF[(min(i, j), max(i, j))]

    lower, inverse = cholesky(lambda i, j: ahead[pair(i, j), 0], 4)
    x = [0.5 * v * valid for v in substitute(lower, inverse, gradient, 4)]
    for _ in range(ITERS - 1):
        misfit = list(gradient)
        for n in range(4):
            up = {t: pltpu.roll(x[n], 128 - t, 1) for t in (1, 2, 3)}
            down = {t: pltpu.roll(x[n], t, 1) for t in (1, 2, 3)}
            for m in range(4):
                p = pair(m, n)
                acc = ahead[p, 0] * x[n]
                for t in (1, 2, 3):
                    acc = acc + ahead[p, t] * up[t] + behind[p, t] * down[t]
                misfit[m] = misfit[m] - acc
            before = jnp.where(k == 0, pltpu.roll(down[1], 1, 0), down[1])
            after = jnp.where(k == KB - 1, pltpu.roll(up[1], 31, 0), up[1])
            misfit[n] = misfit[n] + 16.0 * (before + after)
        x = [(v + 0.5 * w) * valid for v, w in zip(x, substitute(lower, inverse, misfit, 4))]
    sub8 = lax.broadcasted_iota(jnp.int32, (8, 128), 0)
    keep = sub8 == lax.broadcasted_iota(jnp.int32, (8, 128), 1) // KB
    for m in range(4):
        for h in range(2):
            part = jnp.where(keep, x[m][8 + h * 8:16 + h * 8], 0.0)
            out[m:m + 1, h * 128:(h + 1) * 128] = jnp.sum(part, axis=0, keepdims=True)


def per_device(
    attitude, star_partials, attitude_partials, observed, phase, knot_offset, cell_counts, interval_owner, block_slot
):
    dma = pltpu.SemaphoreType.DMA
    owners = interval_owner.reshape(CELLS_HERE, NT)
    pay, codes = pl.pallas_call(
        normal_kernel,
        out_shape=(
            jax.ShapeDtypeStruct((10 * DEV, 128), f32),
            jax.ShapeDtypeStruct((TR, 128), jnp.int32),
        ),
        in_specs=[SMEM, SMEM, SMEM] + [VMEM] * 3,
        out_specs=(VMEM, VMEM),
        scratch_shapes=[
            pltpu.VMEM((10 * TR, 128), f32),
            pltpu.VMEM((4 * TR, 128), f32),
            pltpu.VMEM((TR, 128), jnp.int32),
            pltpu.SMEM((DEV,), jnp.int32),
        ],
        name="normal_terms",
    )(cell_counts, owners, block_slot, attitude_partials, phase, knot_offset)
    peers, column = NP - 1, NZ - 1
    steps, reduced = pl.pallas_call(
        main_kernel,
        out_shape=(
            jax.ShapeDtypeStruct((5, CELLS_HERE * CS), f32),
            jax.ShapeDtypeStruct((6, 32, 128), f32),
        ),
        in_specs=[SMEM, SMEM, SMEM] + [VMEM] * 8,
        out_specs=(VMEM, VMEM),
        scratch_shapes=[
            pltpu.VMEM((NZ, NY, NC, NX, 8, 128), f32),
            pltpu.VMEM((TR * KB, 128), bf16),
            pltpu.VMEM((TR * KB, 128), bf16),
            pltpu.VMEM((32, 128), f32),
            pltpu.VMEM((8, 128), jnp.int32),
            pltpu.VMEM((4 * TR, 128), f32),
            pltpu.VMEM((TR, 128), f32),
            pltpu.VMEM((24, CELLS_HERE * CS), f32),
            pltpu.VMEM((DEV, 2 * TR), bf16),
            pltpu.VMEM((TR, 128), f32),
            pltpu.VMEM((DEV, 128), f32),
            pltpu.VMEM((NP, 10, QIN, 128), f32),
            pltpu.VMEM((NP, QIN, 128), f32),
            pltpu.VMEM((6, QIN * KB, 128), f32),
            pltpu.VMEM((6, NZ * KB, 128), f32),
            pltpu.VMEM((6, NZ * KB, 128), f32),
            pltpu.VMEM((NZ, 6, KB, 128), f32),
            dma((column,)), dma((column,)), dma((peers,)), dma((peers,)), dma, dma,
            dma((peers,)), dma((peers,)), dma((peers,)), dma((peers,)), dma((2,)), dma((2,)),
            dma((column,)), dma((column,)), dma((column,)), dma((column,)), dma((2,)), dma((2,)),
        ],
        compiler_params=pltpu.CompilerParams(collective_id=0, has_side_effects=True),
        name="exchange",
    )(
        cell_counts, owners, block_slot, attitude, pay.reshape(10, DEV, 128), codes,
        star_partials, attitude_partials, observed, phase, knot_offset,
    )
    attitude_step, star_step = pl.pallas_call(
        sweep_kernel,
        out_shape=(
            jax.ShapeDtypeStruct((4, 256), f32),
            jax.ShapeDtypeStruct((5, CELLS_HERE * CS), f32),
        ),
        in_specs=[VMEM, VMEM],
        out_specs=(VMEM, VMEM),
        name="sweeps",
    )(reduced, steps)
    return (star_step, attitude_step)


def solution(mesh):
    both = ("cells", "tm")
    placed = (
        P(None, both), P(None, None, both), P(None, None, both), P(None, both), P(None, both), P(None, both),
        P(both), P(both, None, None), P(both, None),
    )
    return jax.shard_map(
        per_device, mesh=mesh, in_specs=placed, out_specs=(P(None, both), P(None, both)), check_vma=False
    )
```

time: 114 us -> 102 us (0.89)
  the two profiles are of different devices: /device:TPU:26 before, /device:TPU:1 now
where the time goes in v2:
time: 102 us; the launch traced here: 101 us
  Pallas kernels  101 us (99%)
    pallas_call x1, Pallas kernels, per_device(): pl.pallas_call(main_kernel, out_shape=(jax.ShapeDtypeStruct((5, CELLS_HER...  84.1 us
    pallas_call x1, Pallas kernels, per_device(): pl.pallas_call(normal_kernel, out_shape=(jax.ShapeDtypeStruct((10 * DEV,...  13.3 us
    pallas_call x1, Pallas kernels, per_device(): pl.pallas_call(sweep_kernel, out_shape=(jax.ShapeDtypeStruct((4, 256), f3...  3.36 us

profile of v2, /device:TPU:1, one launch (start us, length us, event | category | flops | bytes accessed | tf_op | source)
XLA Modules:
  0.0 101.4 jit_solution(14662309138570087600)
XLA Ops:
  0.6 13.3 %normal_terms.1 = (f32[2560,128]{1,0:T(8,128)}, s32[256,128]{1,0:T(8,128)}) custom-call(s32[4]{0:T(128)} %counts.3, s32[4,64]{1,0:T(4,128)} %bitcast.3, s32[4,64]{1,0:T(4,128)} %slots.3, f32[4,64,512]{2,1,0:T(8,128)} %axis.3, f32[64,512]{1,0:T(8,128)} %phase.3, s32[64,512]{1,0:T(8,128)} %offset.3), custom_call_target="tpu_custom_call" | custom-call | tf_op jit(solution)/shard_map/normal_terms/pallas_call | solution.py:499
  14.0 84.1 %exchange.1 = (f32[5,512]{1,0:T(8,128)}, f32[6,32,128]{2,1,0:T(8,128)}) custom-call(s32[4]{0:T(128)} %counts.3, s32[4,64]{1,0:T(4,128)} %bitcast.4, s32[4,64]{1,0:T(4,128)} %slots.3, f32[4,256]{1,0:T(4,128)} %att_in.1, f32[10,256,128]{2,1,0:T(8,128)} %bitcast.2, s32[256,128]{1,0:T(8,128)} %get-tuple-element.9.codes, f32[5,64,512]{2,1,0:T(8,128)} %star.1, ...), custom_call_target="tpu_custom_call" | custom-call | tf_op jit(solution)/shard_map/exchange/pallas_call | solution.py:516
  98.1 3.4 %sweeps.1 = (f32[4,256]{1,0:T(4,128)}, f32[5,512]{1,0:T(8,128)}) custom-call(f32[6,32,128]{2,1,0:T(8,128)} %get-tuple-element.10.red, f32[5,512]{1,0:T(8,128)} %get-tuple-element.11.steps), custom_call_target="tpu_custom_call" | custom-call | tf_op jit(solution)/shard_map/sweeps/pallas_call | solution.py:552

commit v3 on v2

--- a/solution.py
+++ b/solution.py
@@ -58,7 +58,7 @@
     barrier = pltpu.get_barrier_semaphore()
     for target in targets:
         pl.semaphore_signal(barrier, inc=1, device_id=target, device_id_type=MESH)
-    pl.semaphore_wait(barrier, len(targets))
+    return lambda: pl.semaphore_wait(barrier, len(targets))
 
 
 def split(value):
@@ -126,40 +126,82 @@
     return pl.multiple_of(value, 8)
 
 
-def normal_kernel(counts, owners, slots, axis, phase, offset, pay, codes, cross, parts, offs, used):
+def main_kernel(
+    counts, owners, slots, att_in, star, axis, observed, phase, offset,
+    step_ref, out,
+    att, cross, parts, offs, ownm, nrm, pay, sh, sl, table, first, sums, order, pick, grads, gpay, got, ggot,
+    comb, part, zsum, zgot,
+    zs, zr, ps, pr, cs, cr, ns, nr, gs, gr, ws, wr, us, ur, hs, hr,
+):
+    x, y, z, c = place()
+    plane, column = plane_peers(x, y, z, c), column_peers(x, y, z, c)
+    partner = device(x, y, z, 1 - c)
+    rank = ((z * NY + y) * NC + c) * NX + x
+    after, before = (rank + 1) % DEV, (rank + DEV - 1) % DEV
+    right, left = (after // NX, after % NX), (before // NX, before % NX)
+    all_here = greet([t for _, t in plane] + [t for _, t in column] + [partner, right, left])
+    here = x * NY + y
+    spot = (y * NC + c) * NX + x
+
     sub8 = lax.broadcasted_iota(jnp.int32, (8, 128), 0)
     lane8 = lax.broadcasted_iota(jnp.int32, (8, 128), 1)
-
-    def clear(i, carry):
-        pay[pl.ds(aligned(i * 128), 128), :] = jnp.zeros((128, 128), f32)
-        return carry
-
-    lax.fori_loop(0, 10 * DEV // 128, clear, 0)
-    for c in range(CELLS_HERE):
-        lanes = slice(c * CS, (c + 1) * CS)
-
-        def prepare(g, carry, c=c, lanes=lanes):
+    knot = lax.broadcasted_iota(jnp.int32, (16, 128), 0)
+    att[z, spot, 0:4, :] = att_in[:, 0:128]
+    att[z, spot, 4:8, :] = att_in[:, 128:256]
+
+    for cell in range(CELLS_HERE):
+        lanes = slice(cell * CS, (cell + 1) * CS)
+
+        def prepare(g, acc, cell=cell, lanes=lanes):
             rows = pl.ds(aligned(g * 8), 8)
-            here = c * NT + g * 8
-            live = jnp.where(sub8 + g * 8 < counts[c], 1.0, 0.0)
+            at = cell * NT + g * 8
+            live = jnp.where(sub8 + g * 8 < counts[cell], 1.0, 0.0)
             b = spline(phase[rows, lanes], live)
-            offs[pl.ds(aligned(here), 8), :] = offset[rows, lanes]
+            offs[pl.ds(aligned(at), 8), :] = offset[rows, lanes]
             for n, (shift, i) in enumerate(SHIFTS):
-                cross[pl.ds(aligned(n * TR + here), 8), :] = b[i] * b[i + shift]
+                cross[pl.ds(aligned(n * TR + at), 8), :] = b[i] * b[i + shift]
             for m in range(4):
-                parts[pl.ds(aligned(m * TR + here), 8), :] = axis[m, rows, lanes]
-            for i in range(8):
-                used[here + i] = 0
-            return carry
-
-        lax.fori_loop(0, NT // 8, prepare, 0)
-
-    knot = lax.broadcasted_iota(jnp.int32, (16, 128), 0)
-
-    def normals(g, carry):
-        c, base = lax.shift_right_logical(g, 3), (g & 7) * 8
+                parts[pl.ds(aligned(m * TR + at), 8), :] = axis[m, rows, lanes]
+                parts[pl.ds(aligned((4 + m) * TR + at), 8), :] = b[m]
+            for jj in range(8):
+                ownm[pl.ds(at + jj, 1), :] = jnp.full((1, 128), owners[cell, g * 8 + jj], jnp.int32)
+            p = [star[m, rows, lanes] * live for m in range(5)]
+            terms = [p[i] * p[j] for i in range(5) for j in range(i + 1)]
+            return tuple(s + term for s, term in zip(acc, terms))
+
+        acc = lax.fori_loop(0, NT // 8, prepare, tuple(jnp.zeros((8, 128), f32) for _ in range(15)))
+        for n in range(15):
+            sums[n:n + 1, lanes] = jnp.sum(acc[n], axis=0, keepdims=True)
+
+    def spreads(g, carry):
+        pieces = []
         for jj in range(8):
             at = g * 8 + jj
+            gap = knot - jnp.broadcast_to(offs[pl.ds(at, 1), :], (16, 128))
+            pieces.append(spread([parts[pl.ds((4 + i) * TR + at, 1), :] for i in range(4)], [gap == i for i in range(4)]))
+        high, low = split(jnp.concatenate(pieces, axis=0))
+        where = pl.ds(pl.multiple_of(g * 128, 128), 128)
+        sh[where, :] = high
+        sl[where, :] = low
+        return carry
+
+    lax.fori_loop(0, TR // 8, spreads, 0)
+
+    def entry(i, j):
+        n = i * (i + 1) // 2 + j
+        return sums[n:n + 1, :] + (1.0 if i == j else 0.0)
+
+    lower, inverse = cholesky(entry, 5)
+
+    all_here()
+    mine = att.at[z, spot]
+    gather_z = [remote(mine, mine, zs.at[i], zr.at[i], t) for i, (_, t) in enumerate(column)]
+    for copy in gather_z:
+        copy.start()
+
+    def normals(g, carry):
+        for jj in range(16):
+            at = g * 16 + jj
             gap = knot - jnp.broadcast_to(offs[pl.ds(at, 1), :], (16, 128))
             hits = [gap == i for i in range(4)]
             right = jnp.concatenate(
@@ -178,112 +220,67 @@
             )
             rh, rl = split(right)
             lh, ll = split(jnp.concatenate([top, bottom], axis=0))
-            out = nt_dot(jnp.concatenate([lh, ll], axis=0), jnp.concatenate([rh, rl], axis=0))
-            total = out[0:16] + out[16:32]
+            big = nt_dot(jnp.concatenate([lh, ll], axis=0), jnp.concatenate([rh, rl], axis=0))
+            total = big[0:16] + big[16:32]
             total = total + pltpu.roll(total, 64, 1)
             packed = jnp.where(lane8 < 64, total[0:8], total[8:16])
-            owner, slot = owners[c, base + jj], slots[c, base + jj]
-            rank = used[owner]
-            used[owner] = rank + 1
-            plane = ((owner & 3) << 2) | ((owner >> 3) & 3)
-            q = (plane << 4) | ((owner & 4) << 1) | (owner >> 5)
+            slot = slots[lax.shift_right_logical(g, 2), (g & 3) * 16 + jj]
             packed = jnp.where((sub8 == 0) & (lane8 == ID_LANE), slot.astype(f32), packed)
-            pay[pl.ds(rank * (5 * DEV) + q, 5, stride=DEV), :] = packed[0:5]
-            codes[pl.ds(at, 1), :] = jnp.full((1, 128), rank * DEV + q, jnp.int32)
+            nrm[pl.ds(at, 5, stride=TR), :] = packed[0:5]
         return carry
 
-    lax.fori_loop(0, TR // 8, normals, 0)
-
-
-def main_kernel(
-    counts, owners, slots, att_in, pay, codes, star, axis, observed, phase, offset,
-    step_ref, out,
-    att, sh, sl, tile, otile, table, first, sums, order, grads, gpay, got, ggot, comb, part, zsum, zgot,
-    zs, zr, ps, pr, cs, cr, ns, nr, gs, gr, ws, wr, us, ur, vs, vr, hs, hr,
-):
-    x, y, z, c = place()
-    plane, column = plane_peers(x, y, z, c), column_peers(x, y, z, c)
-    partner = device(x, y, z, 1 - c)
-    rank = ((z * NY + y) * NC + c) * NX + x
-    after, before = (rank + 1) % DEV, (rank + DEV - 1) % DEV
-    right, left = (after // NX, after % NX), (before // NX, before % NX)
-    greet([t for _, t in plane] + [t for _, t in column] + [partner, right, left])
-    here = x * NY + y
-    sent = []
-
-    att[z, y, c, x, 0:4, :] = att_in[:, 0:128]
-    att[z, y, c, x, 4:8, :] = att_in[:, 128:256]
-    mine = att.at[z, y, c, x]
-    gather_z = [remote(mine, mine, zs.at[i], zr.at[i], t) for i, (_, t) in enumerate(column)]
-    for copy in gather_z:
-        copy.start()
-
-    sub8 = lax.broadcasted_iota(jnp.int32, (8, 128), 0)
-    lane8 = lax.broadcasted_iota(jnp.int32, (8, 128), 1)
-    knot = lax.broadcasted_iota(jnp.int32, (16, 128), 0)
-
-    def spreads(cell):
-        lanes = slice(cell * CS, (cell + 1) * CS)
-
-        def body(g, acc):
-            rows = pl.ds(aligned(g * 8), 8)
-            live = jnp.where(sub8 + g * 8 < counts[cell], 1.0, 0.0)
-            b = spline(phase[rows, lanes], live)
-            otile[...] = offset[rows, lanes]
-            for i in range(4):
-                tile[i * 8:(i + 1) * 8, :] = b[i]
-            pieces = []
-            for jj in range(8):
-                gap = knot - jnp.broadcast_to(otile[jj:jj + 1, :], (16, 128))
-                pieces.append(spread([tile[i * 8 + jj:i * 8 + jj + 1, :] for i in range(4)], [gap == i for i in range(4)]))
-            high, low = split(jnp.concatenate(pieces, axis=0))
-            where = pl.ds(pl.multiple_of((cell * 8 + g) * 128, 128), 128)
-            sh[where, :] = high
-            sl[where, :] = low
-            p = [star[m, rows, lanes] * live for m in range(5)]
-            terms = [p[i] * p[j] for i in range(5) for j in range(i + 1)]
-            return tuple(s + term for s, term in zip(acc, terms))
-
-        acc = lax.fori_loop(0, NT // 8, body, tuple(jnp.zeros((8, 128), f32) for _ in range(15)))
-        for n in range(15):
-            sums[n:n + 1, lanes] = jnp.sum(acc[n], axis=0, keepdims=True)
-
-    spreads(0)
-    spreads(1)
+    lax.fori_loop(0, 7, normals, 0)
 
     for copy in gather_z:
         copy.wait_recv()
-    mine = att.at[:, y, c, x]
+    mine = att.at[:, spot]
     gather_p = [remote(mine, mine, ps.at[i], pr.at[i], t) for i, (_, t) in enumerate(plane)]
     for copy in gather_p:
         copy.start()
-    terms = [
-        remote(pay.at[:, pl.ds(p * QIN, QIN), :], got.at[here], ns.at[i], nr.at[i], t)
-        for i, (p, t) in enumerate(plane)
-    ]
-    for copy in terms:
-        copy.start()
-    got[here] = pay[:, pl.ds(pl.multiple_of(here * QIN, QIN), QIN), :]
-
-    spreads(2)
-    spreads(3)
-
-    def entry(i, j):
-        n = i * (i + 1) // 2 + j
-        return sums[n:n + 1, :] + (1.0 if i == j else 0.0)
-
-    lower, inverse = cholesky(entry, 5)
+
+    lax.fori_loop(7, TR // 16, normals, 0)
+
+    owner = jnp.concatenate([ownm[...], ownm[...]], axis=1)
+    other = owner.astype(f32).T
+    left_of = lax.broadcasted_iota(jnp.int32, (TR, TR), 1) < lax.broadcasted_iota(jnp.int32, (TR, TR), 0)
+    same = jnp.where((owner.astype(f32) == other) & left_of, 1.0, 0.0)
+    place_in = jnp.sum(same, axis=1, keepdims=True).astype(jnp.int32)
+    q = ((owner & 3) << 6) | ((owner & 24) << 1) | ((owner & 4) << 1) | lax.shift_right_logical(owner, 5)
+    code = q + place_in * DEV
     target = lax.broadcasted_iota(jnp.int32, (TR, DEV), 1)
-    code = jnp.broadcast_to(codes[:, 0:1], (TR, DEV))
     for s in range(2):
-        order[:, s * TR:(s + 1) * TR] = jnp.where(code == target + s * DEV, 1.0, 0.0).T.astype(bf16)
+        order[s * DEV:(s + 1) * DEV, :] = jnp.where(code == target + s * DEV, 1.0, 0.0).T.astype(bf16)
+
+    def doubled(matrix, data):
+        big = jnp.dot(matrix, jnp.concatenate(split(data), axis=1), preferred_element_type=f32)
+        return big[:, 0:128] + big[:, 128:256]
+
+    for r in range(5):
+        sorted_rows = doubled(order[...], nrm[r * TR:(r + 1) * TR, :])
+        for s in range(2):
+            pay[r, s] = sorted_rows[s * DEV:(s + 1) * DEV]
 
     for copy in gather_p:
         copy.wait_recv()
-    mine = att.at[:, :, c]
-    gather_c = remote(mine, mine, cs, cr, partner)
-    gather_c.start()
-    gather_c.wait_recv()
+    gather_c = []
+    for i in range(NY):
+        mine = att.at[:, pl.ds(i * NC * NX + c * NX, NX)]
+        gather_c.append(remote(mine, mine, cs.at[i], cr.at[i], partner))
+    for copy in gather_c:
+        copy.start()
+    terms = [
+        [
+            remote(pay.at[r, :, pl.ds(p * QIN, QIN), :], got.at[r, here], ns.at[r, i], nr.at[r, i], t)
+            for i, (p, t) in enumerate(plane)
+        ]
+        for r in range(5)
+    ]
+    for group in terms:
+        for copy in group:
+            copy.start()
+    got[:, here] = pay[:, :, pl.ds(pl.multiple_of(here * QIN, QIN), QIN), :]
+    for copy in gather_c:
+        copy.wait_recv()
 
     lane4 = lax.broadcasted_iota(jnp.int32, (4, 128), 1) // KB
 
@@ -291,7 +288,7 @@
         cell, base = lax.shift_right_logical(g, 3), (g & 7) * 8
         for jj in range(8):
             owner, slot = owners[cell, base + jj], slots[cell, base + jj]
-            rows4 = att[owner >> 5, (owner >> 3) & 3, (owner >> 2) & 1, owner & 3, pl.ds((slot >> 3) * 4, 4), :]
+            rows4 = att[lax.shift_right_logical(owner, 5), owner & 31, pl.ds((slot & 8) >> 1, 4), :]
             table[pl.ds(g * 32 + jj, 4, stride=8), :] = jnp.where(lane4 == (slot & 7), rows4, 0.0)
         return carry
 
@@ -324,7 +321,7 @@
             first[pl.ds(aligned(gg * 8), 8), :] = value
             return tuple(s + star[n, rows, lanes] * value for n, s in enumerate(acc))
 
-        acc = lax.fori_loop(0, NT // 8, predict, tuple(jnp.zeros((8, 128), f32) for _ in range(5)))
+        acc = lax.fori_loop(0, NT // 8, predict, tuple(jnp.zeros((8, 128), f32) for _ in range(5)), unroll=2)
         for n in range(5):
             sums[15 + n:16 + n, lanes] = jnp.sum(acc[n], axis=0, keepdims=True)
 
@@ -354,17 +351,11 @@
             grads[pl.ds(aligned(gg * 8), 8), :] = grad
             return carry
 
-        lax.fori_loop(0, NT // 8, gradients, 0)
+        lax.fori_loop(0, NT // 8, gradients, 0, unroll=2)
 
     lane = lax.broadcasted_iota(jnp.int32, (TR, 128), 1)
-
-    def halves(both):
-        return split(jnp.concatenate([jnp.where(lane < 64, both, 0.0), jnp.where(lane < 64, 0.0, both)], axis=0))
-
-    high, low = halves(grads[...])
-    gpay[...] = jnp.dot(order[...], high, preferred_element_type=f32) + jnp.dot(
-        order[...], low, preferred_element_type=f32
-    )
+    placed = doubled(order[...], grads[...])
+    gpay[...] = jnp.where(lane < 64, placed[0:DEV], placed[DEV:2 * DEV])
     gterms = [
         remote(gpay.at[pl.ds(p * QIN, QIN), :], ggot.at[here], gs.at[i], gr.at[i], t) for i, (p, t) in enumerate(plane)
     ]
@@ -372,66 +363,62 @@
         copy.start()
     ggot[here] = gpay[pl.ds(pl.multiple_of(here * QIN, QIN), QIN), :]
 
-    for copy in terms:
-        copy.wait_recv()
     rows = NP * QIN
     cols = QIN * KB
-    row = lax.broadcasted_iota(jnp.int32, (rows, cols), 0)
-    col = lax.broadcasted_iota(jnp.int32, (rows, cols), 1)
-    local = (col - (row % QIN) * KB).astype(f32)
-    for s in range(2):
-        ids = got[:, s * 5, :, :].reshape(rows, 128)[:, ID_LANE:ID_LANE + 1]
-        order[:, s * rows:(s + 1) * rows] = jnp.where(local == ids, 1.0, 0.0).T.astype(bf16)
     half = NZ * KB
     keep = pl.ds(pl.multiple_of(c * half, half), half)
     give = pl.ds(pl.multiple_of((1 - c) * half, half), half)
-
-    def combine(r, high, low):
-        comb[r] = jnp.dot(order[...], high, preferred_element_type=f32) + jnp.dot(
-            order[...], low, preferred_element_type=f32
-        )
-
-    for r in range(5):
-        data = jnp.concatenate([got[:, s * 5 + r, :, :].reshape(rows, 128) for s in range(2)], axis=0)
-        combine(r, *split(data))
-    five = pl.ds(0, 5)
-    swap = remote(comb.at[five, give, :], part.at[five], ws.at[0], wr.at[0], partner)
-    swap.start()
-    for copy in gterms:
-        copy.wait_recv()
-    combine(5, *halves(ggot[...].reshape(rows, 128)))
-    gswap = remote(comb.at[5, give, :], part.at[5], ws.at[1], wr.at[1], partner)
-    gswap.start()
-    swap.wait_recv()
-    zsum[0:5] = comb[0:5, keep, :] + part[0:5]
+    swaps = [remote(comb.at[r, give, :], part.at[r], ws.at[r], wr.at[r], partner) for r in range(6)]
     along = [
-        remote(zsum.at[five, pl.ds(zz * KB, KB), :], zgot.at[z, five], us.at[i], ur.at[i], t)
-        for i, (zz, t) in enumerate(column)
+        [
+            remote(zsum.at[r, pl.ds(zz * KB, KB), :], zgot.at[r, z], us.at[r, i], ur.at[r, i], t)
+            for i, (zz, t) in enumerate(column)
+        ]
+        for r in range(6)
     ]
-    for copy in along:
-        copy.start()
-    gswap.wait_recv()
-    zsum[5] = comb[5, keep, :] + part[5]
-    galong = [
-        remote(zsum.at[5, pl.ds(zz * KB, KB), :], zgot.at[z, 5], vs.at[i], vr.at[i], t)
-        for i, (zz, t) in enumerate(column)
-    ]
-    for copy in galong:
-        copy.start()
-    zgot[z] = zsum[:, pl.ds(pl.multiple_of(z * KB, KB), KB), :]
-    for copy in along + galong:
-        copy.wait_recv()
-    total = zgot[0]
-    for i in range(1, NZ):
-        total = total + zgot[i]
-    out[:, 8:24, :] = total
+
+    def forward(r):
+        swaps[r].wait_recv()
+        zsum[r] = comb[r, keep, :] + part[r]
+        for copy in along[r]:
+            copy.start()
+        zgot[r, z] = zsum[r, pl.ds(pl.multiple_of(z * KB, KB), KB), :]
+
+    for r in range(6):
+        for copy in terms[r] if r < 5 else gterms:
+            copy.wait_recv()
+        if r == 0:
+            row = lax.broadcasted_iota(jnp.int32, (rows, cols), 0)
+            col = lax.broadcasted_iota(jnp.int32, (rows, cols), 1)
+            local = (col - (row % QIN) * KB).astype(f32)
+            for s in range(2):
+                ids = got[0, :, s, :, :].reshape(rows, 128)[:, ID_LANE:ID_LANE + 1]
+                pick[:, s * rows:(s + 1) * rows] = jnp.where(local == ids, 1.0, 0.0).T.astype(bf16)
+        if r < 5:
+            data = jnp.concatenate([got[r, :, s, :, :].reshape(rows, 128) for s in range(2)], axis=0)
+        else:
+            both = ggot[...].reshape(rows, 128)
+            data = jnp.concatenate([jnp.where(lane < 64, both, 0.0), jnp.where(lane < 64, 0.0, both)], axis=0)
+        comb[r] = doubled(pick[...], data)
+        swaps[r].start()
+        if r > 0:
+            forward(r - 1)
+    forward(5)
+    for group in along:
+        for copy in group:
+            copy.wait_recv()
+    for r in range(6):
+        total = zgot[r, 0]
+        for i in range(1, NZ):
+            total = total + zgot[r, i]
+        out[r, 8:24, :] = total
     halo = [
         remote(out.at[:, 16:24, :], out.at[:, 0:8, :], hs.at[0], hr.at[0], right),
         remote(out.at[:, 8:16, :], out.at[:, 24:32, :], hs.at[1], hr.at[1], left),
     ]
     for copy in halo:
         copy.start()
-    for copy in gather_z + gather_p + [gather_c] + terms + gterms + [swap, gswap] + along + galong:
+    for copy in gather_z + gather_p + gather_c + sum(terms, []) + gterms + swaps + sum(along, []):
         copy.wait_send()
     for copy in halo:
         copy.wait()
@@ -496,22 +483,6 @@
 ):
     dma = pltpu.SemaphoreType.DMA
     owners = interval_owner.reshape(CELLS_HERE, NT)
-    pay, codes = pl.pallas_call(
-        normal_kernel,
-        out_shape=(
-            jax.ShapeDtypeStruct((10 * DEV, 128), f32),
-            jax.ShapeDtypeStruct((TR, 128), jnp.int32),
-        ),
-        in_specs=[SMEM, SMEM, SMEM] + [VMEM] * 3,
-        out_specs=(VMEM, VMEM),
-        scratch_shapes=[
-            pltpu.VMEM((10 * TR, 128), f32),
-            pltpu.VMEM((4 * TR, 128), f32),
-            pltpu.VMEM((TR, 128), jnp.int32),
-            pltpu.SMEM((DEV,), jnp.int32),
-        ],
-        name="normal_terms",
-    )(cell_counts, owners, block_slot, attitude_partials, phase, knot_offset)
     peers, column = NP - 1, NZ - 1
     steps, reduced = pl.pallas_call(
         main_kernel,
@@ -519,34 +490,39 @@
             jax.ShapeDtypeStruct((5, CELLS_HERE * CS), f32),
             jax.ShapeDtypeStruct((6, 32, 128), f32),
         ),
-        in_specs=[SMEM, SMEM, SMEM] + [VMEM] * 8,
+        in_specs=[SMEM, SMEM, SMEM] + [VMEM] * 6,
         out_specs=(VMEM, VMEM),
         scratch_shapes=[
-            pltpu.VMEM((NZ, NY, NC, NX, 8, 128), f32),
+            pltpu.VMEM((NZ, NY * NC * NX, 8, 128), f32),
+            pltpu.VMEM((10 * TR, 128), f32),
+            pltpu.VMEM((8 * TR, 128), f32),
+            pltpu.VMEM((TR, 128), jnp.int32),
+            pltpu.VMEM((TR, 128), jnp.int32),
+            pltpu.VMEM((5 * TR, 128), f32),
+            pltpu.VMEM((5, 2, DEV, 128), f32),
             pltpu.VMEM((TR * KB, 128), bf16),
             pltpu.VMEM((TR * KB, 128), bf16),
-            pltpu.VMEM((32, 128), f32),
-            pltpu.VMEM((8, 128), jnp.int32),
             pltpu.VMEM((4 * TR, 128), f32),
             pltpu.VMEM((TR, 128), f32),
             pltpu.VMEM((24, CELLS_HERE * CS), f32),
-            pltpu.VMEM((DEV, 2 * TR), bf16),
+            pltpu.VMEM((2 * DEV, TR), bf16),
+            pltpu.VMEM((QIN * KB, 2 * NP * QIN), bf16),
             pltpu.VMEM((TR, 128), f32),
             pltpu.VMEM((DEV, 128), f32),
-            pltpu.VMEM((NP, 10, QIN, 128), f32),
+            pltpu.VMEM((5, NP, 2, QIN, 128), f32),
             pltpu.VMEM((NP, QIN, 128), f32),
             pltpu.VMEM((6, QIN * KB, 128), f32),
             pltpu.VMEM((6, NZ * KB, 128), f32),
             pltpu.VMEM((6, NZ * KB, 128), f32),
-            pltpu.VMEM((NZ, 6, KB, 128), f32),
-            dma((column,)), dma((column,)), dma((peers,)), dma((peers,)), dma, dma,
-            dma((peers,)), dma((peers,)), dma((peers,)), dma((peers,)), dma((2,)), dma((2,)),
-            dma((column,)), dma((column,)), dma((column,)), dma((column,)), dma((2,)), dma((2,)),
+            pltpu.VMEM((6, NZ, KB, 128), f32),
+            dma((column,)), dma((column,)), dma((peers,)), dma((peers,)), dma((NY,)), dma((NY,)),
+            dma((5, peers)), dma((5, peers)), dma((peers,)), dma((peers,)), dma((6,)), dma((6,)),
+            dma((6, column)), dma((6, column)), dma((2,)), dma((2,)),
         ],
         compiler_params=pltpu.CompilerParams(collective_id=0, has_side_effects=True),
         name="exchange",
     )(
-        cell_counts, owners, block_slot, attitude, pay.reshape(10, DEV, 128), codes,
+        cell_counts, owners, block_slot, attitude,
         star_partials, attitude_partials, observed, phase, knot_offset,
     )
     attitude_step, star_step = pl.pallas_call(

time: 102 us -> 64.2 us (0.63)
  Pallas kernels: 101 us -> 63.4 us
    pallas_call x1, Pallas kernels: 84.1 us -> 60.1 us  [per_device(): pl.pallas_call(main_kernel, out_shape=(jax.ShapeDtypeStruct((5, CELLS_HER...]
    pallas_call x1 -> x0, Pallas kernels: 13.3 us -> none  [per_device(): pl.pallas_call(normal_kernel, out_shape=(jax.ShapeDtypeStruct((10 * DEV,...]
where the time goes in v3:
time: 64.2 us; the launch traced here: 64.1 us
  Pallas kernels  63.4 us (99%)
    pallas_call x1, Pallas kernels, per_device(): pl.pallas_call(main_kernel, out_shape=(jax.ShapeDtypeStruct((5, CELLS_HER...  60.1 us
    pallas_call x1, Pallas kernels, per_device(): pl.pallas_call(sweep_kernel, out_shape=(jax.ShapeDtypeStruct((4, 256), f3...  3.36 us

profile of v3, /device:TPU:1, one launch (start us, length us, event | category | flops | bytes accessed | tf_op | source)
XLA Modules:
  0.0 64.1 jit_solution(17470332943075264374)
XLA Ops:
  0.6 60.1 %exchange.1 = (f32[5,512]{1,0:T(8,128)}, f32[6,32,128]{2,1,0:T(8,128)}) custom-call(s32[4]{0:T(128)} %counts.1, s32[4,64]{1,0:T(4,128)} %bitcast.1, s32[4,64]{1,0:T(4,128)} %slots.1, f32[4,256]{1,0:T(4,128)} %att_in.1, f32[5,64,512]{2,1,0:T(8,128)} %star.1, f32[4,64,512]{2,1,0:T(8,128)} %axis.1, f32[64,512]{1,0:T(8,128)} %observed.1, f32[64,512]{1,0:T(8,128)} %phase.1, ...), custom_call_target="tpu_custom_call" | custom-call | tf_op jit(solution)/shard_map/exchange/pallas_call | solution.py:487
  60.7 3.4 %sweeps.1 = (f32[4,256]{1,0:T(4,128)}, f32[5,512]{1,0:T(8,128)}) custom-call(f32[6,32,128]{2,1,0:T(8,128)} %get-tuple-element.6.red, f32[5,512]{1,0:T(8,128)} %get-tuple-element.7.steps), custom_call_target="tpu_custom_call" | custom-call | tf_op jit(solution)/shard_map/sweeps/pallas_call | solution.py:528

commit v4 on v3

--- a/solution.py
+++ b/solution.py
@@ -27,7 +27,7 @@
 
 def place():
     cells, x = lax.axis_index("cells"), lax.axis_index("tm")
-    z, y, c = cells // (NY * NC), (cells // NC) % NY, cells % NC
+    z, y, c = lax.div(cells, NY * NC), lax.rem(lax.div(cells, NC), NY), lax.rem(cells, NC)
     return x, y, z, c
 
 
@@ -42,16 +42,13 @@
 
 
 def plane_peers(x, y, z, c):
-    here = x * NY + y
-    peers = []
-    for i in range(1, NP):
-        there = (here + i) % NP
-        peers.append((there, device(there // NY, there % NY, z, c)))
-    return peers
+    xs = [x] + [lax.rem(x + d, NX) for d in range(1, NX)]
+    ys = [y] + [lax.rem(y + d, NY) for d in range(1, NY)]
+    return [(i * NY + j, device(i, j, z, c)) for i in xs for j in ys][1:]
 
 
 def column_peers(x, y, z, c):
-    return [((z + i) % NZ, device(x, y, (z + i) % NZ, c)) for i in range(1, NZ)]
+    return [(zz, device(x, y, zz, c)) for zz in [lax.rem(z + i, NZ) for i in range(1, NZ)]]
 
 
 def greet(targets):
@@ -137,8 +134,8 @@
     plane, column = plane_peers(x, y, z, c), column_peers(x, y, z, c)
     partner = device(x, y, z, 1 - c)
     rank = ((z * NY + y) * NC + c) * NX + x
-    after, before = (rank + 1) % DEV, (rank + DEV - 1) % DEV
-    right, left = (after // NX, after % NX), (before // NX, before % NX)
+    after, before = lax.rem(rank + 1, DEV), lax.rem(rank + DEV - 1, DEV)
+    right, left = [(lax.div(d, NX), lax.rem(d, NX)) for d in (after, before)]
     all_here = greet([t for _, t in plane] + [t for _, t in column] + [partner, right, left])
     here = x * NY + y
     spot = (y * NC + c) * NX + x
@@ -173,6 +170,95 @@
         for n in range(15):
             sums[n:n + 1, lanes] = jnp.sum(acc[n], axis=0, keepdims=True)
 
+    def sides(at):
+        gap = knot - jnp.broadcast_to(offs[pl.ds(at, 1), :], (16, 128))
+        hits = [gap == i for i in range(4)]
+        right = jnp.concatenate(
+            [
+                spread([cross[pl.ds(SHIFT_OF[(s, i)] * TR + at, 1), :] for i in range(4 - s)], hits)
+                for s in range(4)
+            ],
+            axis=0,
+        )
+        a = [jnp.broadcast_to(parts[pl.ds(m * TR + at, 1), :], (8, 128)) for m in range(4)]
+        top = jnp.where(sub8 == 4, a[1], a[0]) * jnp.where(
+            sub8 == 0, a[0], jnp.where(sub8 == 2, a[2], jnp.where(sub8 == 3, a[3], a[1]))
+        )
+        bottom = jnp.where(sub8 < 2, a[1], jnp.where(sub8 == 4, a[3], a[2])) * jnp.where(
+            (sub8 == 0) | (sub8 == 2), a[2], a[3]
+        )
+        rh, rl = split(right)
+        lh, ll = split(jnp.concatenate([top, bottom], axis=0))
+        return jnp.concatenate([lh, ll], axis=0), jnp.concatenate([rh, rl], axis=0)
+
+    def finish(at, slot, big):
+        total = big[0:16] + big[16:32]
+        total = total + pltpu.roll(total, 64, 1)
+        packed = jnp.where(lane8 < 64, total[0:8], total[8:16])
+        packed = jnp.where((sub8 == 0) & (lane8 == ID_LANE), slot.astype(f32), packed)
+        nrm[pl.ds(at, 5, stride=TR), :] = packed[0:5]
+
+    blank = jnp.zeros((32, 128), bf16)
+
+    def normals(g, carry):
+        for jj in range(0, 32, 2):
+            at = g * 32 + jj
+            left0, right0 = sides(at)
+            left1, right1 = sides(at + 1)
+            left = jnp.concatenate(
+                [jnp.concatenate([left0, blank], axis=1), jnp.concatenate([blank, left1], axis=1)], axis=0
+            )
+            big = nt_dot(left, jnp.concatenate([right0, right1], axis=1))
+            for e in range(2):
+                slot = slots[lax.shift_right_logical(g, 1), (g & 1) * 32 + jj + e]
+                finish(at + e, slot, big[e * 32:(e + 1) * 32])
+        return carry
+
+    lax.fori_loop(0, 4, normals, 0)
+
+    all_here()
+    mine = att.at[z, spot]
+    gather_z = [remote(mine, mine, zs.at[i], zr.at[i], t) for i, (_, t) in enumerate(column)]
+    for copy in gather_z:
+        copy.start()
+
+    lax.fori_loop(4, TR // 32, normals, 0)
+
+    owner = jnp.concatenate([ownm[...], ownm[...]], axis=1)
+    other = owner.astype(f32).T
+    left_of = lax.broadcasted_iota(jnp.int32, (TR, TR), 1) < lax.broadcasted_iota(jnp.int32, (TR, TR), 0)
+    same = jnp.where((owner.astype(f32) == other) & left_of, 1.0, 0.0)
+    place_in = jnp.sum(same, axis=1, keepdims=True).astype(jnp.int32)
+    q = ((owner & 3) << 6) | ((owner & 24) << 1) | ((owner & 4) << 1) | lax.shift_right_logical(owner, 5)
+    code = q + place_in * DEV
+    target = lax.broadcasted_iota(jnp.int32, (TR, DEV), 1)
+    for s in range(2):
+        order[s * DEV:(s + 1) * DEV, :] = jnp.where(code == target + s * DEV, 1.0, 0.0).T.astype(bf16)
+
+    for copy in gather_z:
+        copy.wait_recv()
+    mine = att.at[:, spot]
+    gather_p = [remote(mine, mine, ps.at[i], pr.at[i], t) for i, (_, t) in enumerate(plane)]
+    for copy in gather_p:
+        copy.start()
+
+    def doubled(matrix, data):
+        big = jnp.dot(matrix, jnp.concatenate(split(data), axis=1), preferred_element_type=f32)
+        return big[:, 0:128] + big[:, 128:256]
+
+    terms = []
+    for r in range(5):
+        sorted_rows = doubled(order[...], nrm[r * TR:(r + 1) * TR, :])
+        for s in range(2):
+            pay[r, s] = sorted_rows[s * DEV:(s + 1) * DEV]
+        terms.append([
+            remote(pay.at[r, :, pl.ds(p * QIN, QIN), :], got.at[r, here], ns.at[r, i], nr.at[r, i], t)
+            for i, (p, t) in enumerate(plane)
+        ])
+        for copy in terms[r]:
+            copy.start()
+    got[:, here] = pay[:, :, pl.ds(pl.multiple_of(here * QIN, QIN), QIN), :]
+
     def spreads(g, carry):
         pieces = []
         for jj in range(8):
@@ -193,73 +279,6 @@
 
     lower, inverse = cholesky(entry, 5)
 
-    all_here()
-    mine = att.at[z, spot]
-    gather_z = [remote(mine, mine, zs.at[i], zr.at[i], t) for i, (_, t) in enumerate(column)]
-    for copy in gather_z:
-        copy.start()
-
-    def normals(g, carry):
-        for jj in range(16):
-            at = g * 16 + jj
-            gap = knot - jnp.broadcast_to(offs[pl.ds(at, 1), :], (16, 128))
-            hits = [gap == i for i in range(4)]
-            right = jnp.concatenate(
-                [
-                    spread([cross[pl.ds(SHIFT_OF[(s, i)] * TR + at, 1), :] for i in range(4 - s)], hits)
-                    for s in range(4)
-                ],
-                axis=0,
-            )
-            a = [jnp.broadcast_to(parts[pl.ds(m * TR + at, 1), :], (8, 128)) for m in range(4)]
-            top = jnp.where(sub8 == 4, a[1], a[0]) * jnp.where(
-                sub8 == 0, a[0], jnp.where(sub8 == 2, a[2], jnp.where(sub8 == 3, a[3], a[1]))
-            )
-            bottom = jnp.where(sub8 < 2, a[1], jnp.where(sub8 == 4, a[3], a[2])) * jnp.where(
-                (sub8 == 0) | (sub8 == 2), a[2], a[3]
-            )
-            rh, rl = split(right)
-            lh, ll = split(jnp.concatenate([top, bottom], axis=0))
-            big = nt_dot(jnp.concatenate([lh, ll], axis=0), jnp.concatenate([rh, rl], axis=0))
-            total = big[0:16] + big[16:32]
-            total = total + pltpu.roll(total, 64, 1)
-            packed = jnp.where(lane8 < 64, total[0:8], total[8:16])
-            slot = slots[lax.shift_right_logical(g, 2), (g & 3) * 16 + jj]
-            packed = jnp.where((sub8 == 0) & (lane8 == ID_LANE), slot.astype(f32), packed)
-            nrm[pl.ds(at, 5, stride=TR), :] = packed[0:5]
-        return carry
-
-    lax.fori_loop(0, 7, normals, 0)
-
-    for copy in gather_z:
-        copy.wait_recv()
-    mine = att.at[:, spot]
-    gather_p = [remote(mine, mine, ps.at[i], pr.at[i], t) for i, (_, t) in enumerate(plane)]
-    for copy in gather_p:
-        copy.start()
-
-    lax.fori_loop(7, TR // 16, normals, 0)
-
-    owner = jnp.concatenate([ownm[...], ownm[...]], axis=1)
-    other = owner.astype(f32).T
-    left_of = lax.broadcasted_iota(jnp.int32, (TR, TR), 1) < lax.broadcasted_iota(jnp.int32, (TR, TR), 0)
-    same = jnp.where((owner.astype(f32) == other) & left_of, 1.0, 0.0)
-    place_in = jnp.sum(same, axis=1, keepdims=True).astype(jnp.int32)
-    q = ((owner & 3) << 6) | ((owner & 24) << 1) | ((owner & 4) << 1) | lax.shift_right_logical(owner, 5)
-    code = q + place_in * DEV
-    target = lax.broadcasted_iota(jnp.int32, (TR, DEV), 1)
-    for s in range(2):
-        order[s * DEV:(s + 1) * DEV, :] = jnp.where(code == target + s * DEV, 1.0, 0.0).T.astype(bf16)
-
-    def doubled(matrix, data):
-        big = jnp.dot(matrix, jnp.concatenate(split(data), axis=1), preferred_element_type=f32)
-        return big[:, 0:128] + big[:, 128:256]
-
-    for r in range(5):
-        sorted_rows = doubled(order[...], nrm[r * TR:(r + 1) * TR, :])
-        for s in range(2):
-            pay[r, s] = sorted_rows[s * DEV:(s + 1) * DEV]
-
     for copy in gather_p:
         copy.wait_recv()
     gather_c = []
@@ -268,17 +287,6 @@
         gather_c.append(remote(mine, mine, cs.at[i], cr.at[i], partner))
     for copy in gather_c:
         copy.start()
-    terms = [
-        [
-            remote(pay.at[r, :, pl.ds(p * QIN, QIN), :], got.at[r, here], ns.at[r, i], nr.at[r, i], t)
-            for i, (p, t) in enumerate(plane)
-        ]
-        for r in range(5)
-    ]
-    for group in terms:
-        for copy in group:
-            copy.start()
-    got[:, here] = pay[:, :, pl.ds(pl.multiple_of(here * QIN, QIN), QIN), :]
     for copy in gather_c:
         copy.wait_recv()
 

time: 64.2 us -> 66.4 us (1.034)
  Pallas kernels: 63.4 us -> 65.6 us
    pallas_call x1, Pallas kernels: 60.1 us -> 62.3 us  [per_device(): pl.pallas_call(main_kernel, out_shape=(jax.ShapeDtypeStruct((5, CELLS_HER...]
where the time goes in v4:
time: 66.4 us; the launch traced here: 66.3 us
  Pallas kernels  65.6 us (99%)
    pallas_call x1, Pallas kernels, per_device(): pl.pallas_call(main_kernel, out_shape=(jax.ShapeDtypeStruct((5, CELLS_HER...  62.3 us
    pallas_call x1, Pallas kernels, per_device(): pl.pallas_call(sweep_kernel, out_shape=(jax.ShapeDtypeStruct((4, 256), f3...  3.36 us

profile of v4, /device:TPU:1, one launch (start us, length us, event | category | flops | bytes accessed | tf_op | source)
XLA Modules:
  0.0 66.3 jit_solution(14683845570839277301)
XLA Ops:
  0.6 62.3 %exchange.1 = (f32[5,512]{1,0:T(8,128)}, f32[6,32,128]{2,1,0:T(8,128)}) custom-call(s32[4]{0:T(128)} %counts.1, s32[4,64]{1,0:T(4,128)} %bitcast.1, s32[4,64]{1,0:T(4,128)} %slots.1, f32[4,256]{1,0:T(4,128)} %att_in.1, f32[5,64,512]{2,1,0:T(8,128)} %star.1, f32[4,64,512]{2,1,0:T(8,128)} %axis.1, f32[64,512]{1,0:T(8,128)} %observed.1, f32[64,512]{1,0:T(8,128)} %phase.1, ...), custom_call_target="tpu_custom_call" | custom-call | tf_op jit(solution)/shard_map/exchange/pallas_call | solution.py:495
  62.9 3.4 %sweeps.1 = (f32[4,256]{1,0:T(4,128)}, f32[5,512]{1,0:T(8,128)}) custom-call(f32[6,32,128]{2,1,0:T(8,128)} %get-tuple-element.6.red, f32[5,512]{1,0:T(8,128)} %get-tuple-element.7.steps), custom_call_target="tpu_custom_call" | custom-call | tf_op jit(solution)/shard_map/sweeps/pallas_call | solution.py:536

commit v5 on v4

--- a/solution.py
+++ b/solution.py
@@ -15,6 +15,7 @@
 CELLS_HERE = 4
 TR = CELLS_HERE * NT
 ID_LANE = 63
+EARLY = 1
 MESH = pl.DeviceIdType.MESH
 f32, bf16 = jnp.float32, jnp.bfloat16
 PAIRS = [(m, n) for m in range(4) for n in range(m, 4)]
@@ -138,13 +139,13 @@
     right, left = [(lax.div(d, NX), lax.rem(d, NX)) for d in (after, before)]
     all_here = greet([t for _, t in plane] + [t for _, t in column] + [partner, right, left])
     here = x * NY + y
-    spot = (y * NC + c) * NX + x
+    spot = y * NX + x
 
     sub8 = lax.broadcasted_iota(jnp.int32, (8, 128), 0)
     lane8 = lax.broadcasted_iota(jnp.int32, (8, 128), 1)
     knot = lax.broadcasted_iota(jnp.int32, (16, 128), 0)
-    att[z, spot, 0:4, :] = att_in[:, 0:128]
-    att[z, spot, 4:8, :] = att_in[:, 128:256]
+    att[c, z, spot, 0:4, :] = att_in[:, 0:128]
+    att[c, z, spot, 4:8, :] = att_in[:, 128:256]
 
     for cell in range(CELLS_HERE):
         lanes = slice(cell * CS, (cell + 1) * CS)
@@ -217,12 +218,37 @@
     lax.fori_loop(0, 4, normals, 0)
 
     all_here()
-    mine = att.at[z, spot]
-    gather_z = [remote(mine, mine, zs.at[i], zr.at[i], t) for i, (_, t) in enumerate(column)]
-    for copy in gather_z:
-        copy.start()
-
-    lax.fori_loop(4, TR // 32, normals, 0)
+    slab = att.at[c, z, spot]
+    lines = att.at[c, :, spot]
+    sheet = att.at[c, z]
+    near = [remote(slab, slab, zs.at[i], zr.at[i], t) for i, (_, t) in enumerate(column)]
+    wide = [remote(lines, lines, ps.at[i], pr.at[i], t) for i, (_, t) in enumerate(plane)]
+    flat = [remote(slab, slab, ps.at[i], pr.at[i], t) for i, (_, t) in enumerate(plane)]
+    deep = [remote(sheet, sheet, zs.at[i], zr.at[i], t) for i, (_, t) in enumerate(column)]
+
+    def start_all(copies):
+        for copy in copies:
+            copy.start()
+
+    def arrive(copies):
+        for copy in copies:
+            copy.wait_recv()
+
+    def leave(copies):
+        for copy in copies:
+            copy.wait_send()
+
+    pl.when(c == 0)(lambda: start_all(near))
+    pl.when(c == 1)(lambda: start_all(flat))
+
+    lax.fori_loop(4, 6, normals, 0)
+
+    @pl.when(c == 1)
+    def _():
+        arrive(flat)
+        start_all(deep)
+
+    lax.fori_loop(6, TR // 32, normals, 0)
 
     owner = jnp.concatenate([ownm[...], ownm[...]], axis=1)
     other = owner.astype(f32).T
@@ -235,12 +261,10 @@
     for s in range(2):
         order[s * DEV:(s + 1) * DEV, :] = jnp.where(code == target + s * DEV, 1.0, 0.0).T.astype(bf16)
 
-    for copy in gather_z:
-        copy.wait_recv()
-    mine = att.at[:, spot]
-    gather_p = [remote(mine, mine, ps.at[i], pr.at[i], t) for i, (_, t) in enumerate(plane)]
-    for copy in gather_p:
-        copy.start()
+    @pl.when(c == 0)
+    def _():
+        arrive(near)
+        start_all(wide)
 
     def doubled(matrix, data):
         big = jnp.dot(matrix, jnp.concatenate(split(data), axis=1), preferred_element_type=f32)
@@ -255,8 +279,8 @@
             remote(pay.at[r, :, pl.ds(p * QIN, QIN), :], got.at[r, here], ns.at[r, i], nr.at[r, i], t)
             for i, (p, t) in enumerate(plane)
         ])
-        for copy in terms[r]:
-            copy.start()
+        if r < EARLY:
+            start_all(terms[r])
     got[:, here] = pay[:, :, pl.ds(pl.multiple_of(here * QIN, QIN), QIN), :]
 
     def spreads(g, carry):
@@ -279,16 +303,14 @@
 
     lower, inverse = cholesky(entry, 5)
 
-    for copy in gather_p:
-        copy.wait_recv()
-    gather_c = []
-    for i in range(NY):
-        mine = att.at[:, pl.ds(i * NC * NX + c * NX, NX)]
-        gather_c.append(remote(mine, mine, cs.at[i], cr.at[i], partner))
-    for copy in gather_c:
-        copy.start()
-    for copy in gather_c:
-        copy.wait_recv()
+    pl.when(c == 0)(lambda: arrive(wide))
+    pl.when(c == 1)(lambda: arrive(deep))
+    whole = att.at[c]
+    gather_c = remote(whole, whole, cs, cr, partner)
+    gather_c.start()
+    for r in range(EARLY, 5):
+        start_all(terms[r])
+    gather_c.wait_recv()
 
     lane4 = lax.broadcasted_iota(jnp.int32, (4, 128), 1) // KB
 
@@ -296,7 +318,10 @@
         cell, base = lax.shift_right_logical(g, 3), (g & 7) * 8
         for jj in range(8):
             owner, slot = owners[cell, base + jj], slots[cell, base + jj]
-            rows4 = att[lax.shift_right_logical(owner, 5), owner & 31, pl.ds((slot & 8) >> 1, 4), :]
+            rows4 = att[
+                lax.shift_right_logical(owner & 4, 2), lax.shift_right_logical(owner, 5),
+                ((owner & 24) >> 1) | (owner & 3), pl.ds((slot & 8) >> 1, 4), :
+            ]
             table[pl.ds(g * 32 + jj, 4, stride=8), :] = jnp.where(lane4 == (slot & 7), rows4, 0.0)
         return carry
 
@@ -329,7 +354,7 @@
             first[pl.ds(aligned(gg * 8), 8), :] = value
             return tuple(s + star[n, rows, lanes] * value for n, s in enumerate(acc))
 
-        acc = lax.fori_loop(0, NT // 8, predict, tuple(jnp.zeros((8, 128), f32) for _ in range(5)), unroll=2)
+        acc = lax.fori_loop(0, NT // 8, predict, tuple(jnp.zeros((8, 128), f32) for _ in range(5)), unroll=4)
         for n in range(5):
             sums[15 + n:16 + n, lanes] = jnp.sum(acc[n], axis=0, keepdims=True)
 
@@ -359,7 +384,7 @@
             grads[pl.ds(aligned(gg * 8), 8), :] = grad
             return carry
 
-        lax.fori_loop(0, NT // 8, gradients, 0, unroll=2)
+        lax.fori_loop(0, NT // 8, gradients, 0, unroll=4)
 
     lane = lax.broadcasted_iota(jnp.int32, (TR, 128), 1)
     placed = doubled(order[...], grads[...])
@@ -426,8 +451,9 @@
     ]
     for copy in halo:
         copy.start()
-    for copy in gather_z + gather_p + gather_c + sum(terms, []) + gterms + swaps + sum(along, []):
-        copy.wait_send()
+    pl.when(c == 0)(lambda: leave(near + wide))
+    pl.when(c == 1)(lambda: leave(flat + deep))
+    leave([gather_c] + sum(terms, []) + gterms + swaps + sum(along, []))
     for copy in halo:
         copy.wait()
 
@@ -501,7 +527,7 @@
         in_specs=[SMEM, SMEM, SMEM] + [VMEM] * 6,
         out_specs=(VMEM, VMEM),
         scratch_shapes=[
-            pltpu.VMEM((NZ, NY * NC * NX, 8, 128), f32),
+            pltpu.VMEM((NC, NZ, NY * NX, 8, 128), f32),
             pltpu.VMEM((10 * TR, 128), f32),
             pltpu.VMEM((8 * TR, 128), f32),
             pltpu.VMEM((TR, 128), jnp.int32),
@@ -523,7 +549,7 @@
             pltpu.VMEM((6, NZ * KB, 128), f32),
             pltpu.VMEM((6, NZ * KB, 128), f32),
             pltpu.VMEM((6, NZ, KB, 128), f32),
-            dma((column,)), dma((column,)), dma((peers,)), dma((peers,)), dma((NY,)), dma((NY,)),
+            dma((column,)), dma((column,)), dma((peers,)), dma((peers,)), dma, dma,
             dma((5, peers)), dma((5, peers)), dma((peers,)), dma((peers,)), dma((6,)), dma((6,)),
             dma((6, column)), dma((6, column)), dma((2,)), dma((2,)),
         ],

time: 66.4 us -> 59.4 us (0.89)
  Pallas kernels: 65.6 us -> 58.6 us
    pallas_call x1, Pallas kernels: 62.3 us -> 55.2 us  [per_device(): pl.pallas_call(main_kernel, out_shape=(jax.ShapeDtypeStruct((5, CELLS_HER...]
where the time goes in v5:
time: 59.4 us; the launch traced here: 59.2 us
  Pallas kernels  58.6 us (99%)
  between operations  0.64 us (1%)
    pallas_call x1, Pallas kernels, per_device(): pl.pallas_call(main_kernel, out_shape=(jax.ShapeDtypeStruct((5, CELLS_HER...  55.2 us
    pallas_call x1, Pallas kernels, per_device(): pl.pallas_call(sweep_kernel, out_shape=(jax.ShapeDtypeStruct((4, 256), f3...  3.36 us

profile of v5, /device:TPU:1, one launch (start us, length us, event | category | flops | bytes accessed | tf_op | source)
XLA Modules:
  0.0 59.2 jit_solution(13569532259344778319)
XLA Ops:
  0.6 55.2 %exchange.1 = (f32[5,512]{1,0:T(8,128)}, f32[6,32,128]{2,1,0:T(8,128)}) custom-call(s32[4]{0:T(128)} %counts.1, s32[4,64]{1,0:T(4,128)} %bitcast.1, s32[4,64]{1,0:T(4,128)} %slots.1, f32[4,256]{1,0:T(4,128)} %att_in.1, f32[5,64,512]{2,1,0:T(8,128)} %star.1, f32[4,64,512]{2,1,0:T(8,128)} %axis.1, f32[64,512]{1,0:T(8,128)} %observed.1, f32[64,512]{1,0:T(8,128)} %phase.1, ...), custom_call_target="tpu_custom_call" | custom-call | tf_op jit(solution)/shard_map/exchange/pallas_call | solution.py:521
  55.9 3.4 %sweeps.1 = (f32[4,256]{1,0:T(4,128)}, f32[5,512]{1,0:T(8,128)}) custom-call(f32[6,32,128]{2,1,0:T(8,128)} %get-tuple-element.6.red, f32[5,512]{1,0:T(8,128)} %get-tuple-element.7.steps), custom_call_target="tpu_custom_call" | custom-call | tf_op jit(solution)/shard_map/sweeps/pallas_call | solution.py:562

commit v6 on v5

--- a/solution.py
+++ b/solution.py
@@ -15,7 +15,7 @@
 CELLS_HERE = 4
 TR = CELLS_HERE * NT
 ID_LANE = 63
-EARLY = 1
+EARLY = 2
 MESH = pl.DeviceIdType.MESH
 f32, bf16 = jnp.float32, jnp.bfloat16
 PAIRS = [(m, n) for m in range(4) for n in range(m, 4)]
@@ -127,7 +127,7 @@
 def main_kernel(
     counts, owners, slots, att_in, star, axis, observed, phase, offset,
     step_ref, out,
-    att, cross, parts, offs, ownm, nrm, pay, sh, sl, table, first, sums, order, pick, grads, gpay, got, ggot,
+    att, found, cross, parts, offs, ownm, nrm, pay, sh, sl, table, first, sums, order, pick, grads, gpay, got, ggot,
     comb, part, zsum, zgot,
     zs, zr, ps, pr, cs, cr, ns, nr, gs, gr, ws, wr, us, ur, hs, hr,
 ):
@@ -144,8 +144,8 @@
     sub8 = lax.broadcasted_iota(jnp.int32, (8, 128), 0)
     lane8 = lax.broadcasted_iota(jnp.int32, (8, 128), 1)
     knot = lax.broadcasted_iota(jnp.int32, (16, 128), 0)
-    att[c, z, spot, 0:4, :] = att_in[:, 0:128]
-    att[c, z, spot, 4:8, :] = att_in[:, 128:256]
+    att[c * NZ + z, spot, 0:4, :] = att_in[:, 0:128]
+    att[c * NZ + z, spot, 4:8, :] = att_in[:, 128:256]
 
     for cell in range(CELLS_HERE):
         lanes = slice(cell * CS, (cell + 1) * CS)
@@ -213,14 +213,19 @@
             for e in range(2):
                 slot = slots[lax.shift_right_logical(g, 1), (g & 1) * 32 + jj + e]
                 finish(at + e, slot, big[e * 32:(e + 1) * 32])
+                owner = owners[lax.shift_right_logical(g, 1), (g & 1) * 32 + jj + e]
+                found[0, at + e] = ((owner & 4) << 1) | lax.shift_right_logical(owner, 5)
+                found[1, at + e] = lax.shift_right_logical(owner & 24, 1) | (owner & 3)
+                found[2, at + e] = lax.shift_right_logical(slot & 8, 1)
+                found[3, at + e] = slot & 7
         return carry
 
     lax.fori_loop(0, 4, normals, 0)
 
     all_here()
-    slab = att.at[c, z, spot]
-    lines = att.at[c, :, spot]
-    sheet = att.at[c, z]
+    slab = att.at[c * NZ + z, spot]
+    lines = att.at[pl.ds(c * NZ, NZ), spot]
+    sheet = att.at[c * NZ + z]
     near = [remote(slab, slab, zs.at[i], zr.at[i], t) for i, (_, t) in enumerate(column)]
     wide = [remote(lines, lines, ps.at[i], pr.at[i], t) for i, (_, t) in enumerate(plane)]
     flat = [remote(slab, slab, ps.at[i], pr.at[i], t) for i, (_, t) in enumerate(plane)]
@@ -305,7 +310,7 @@
 
     pl.when(c == 0)(lambda: arrive(wide))
     pl.when(c == 1)(lambda: arrive(deep))
-    whole = att.at[c]
+    whole = att.at[pl.ds(c * NZ, NZ)]
     gather_c = remote(whole, whole, cs, cr, partner)
     gather_c.start()
     for r in range(EARLY, 5):
@@ -315,14 +320,10 @@
     lane4 = lax.broadcasted_iota(jnp.int32, (4, 128), 1) // KB
 
     def choose(g, carry):
-        cell, base = lax.shift_right_logical(g, 3), (g & 7) * 8
         for jj in range(8):
-            owner, slot = owners[cell, base + jj], slots[cell, base + jj]
-            rows4 = att[
-                lax.shift_right_logical(owner & 4, 2), lax.shift_right_logical(owner, 5),
-                ((owner & 24) >> 1) | (owner & 3), pl.ds((slot & 8) >> 1, 4), :
-            ]
-            table[pl.ds(g * 32 + jj, 4, stride=8), :] = jnp.where(lane4 == (slot & 7), rows4, 0.0)
+            at = g * 8 + jj
+            rows4 = att[found[0, at], found[1, at], pl.ds(found[2, at], 4), :]
+            table[pl.ds(g * 32 + jj, 4, stride=8), :] = jnp.where(lane4 == found[3, at], rows4, 0.0)
         return carry
 
     lax.fori_loop(0, TR // 8, choose, 0)
@@ -354,7 +355,7 @@
             first[pl.ds(aligned(gg * 8), 8), :] = value
             return tuple(s + star[n, rows, lanes] * value for n, s in enumerate(acc))
 
-        acc = lax.fori_loop(0, NT // 8, predict, tuple(jnp.zeros((8, 128), f32) for _ in range(5)), unroll=4)
+        acc = lax.fori_loop(0, NT // 8, predict, tuple(jnp.zeros((8, 128), f32) for _ in range(5)), unroll=8)
         for n in range(5):
             sums[15 + n:16 + n, lanes] = jnp.sum(acc[n], axis=0, keepdims=True)
 
@@ -384,7 +385,7 @@
             grads[pl.ds(aligned(gg * 8), 8), :] = grad
             return carry
 
-        lax.fori_loop(0, NT // 8, gradients, 0, unroll=4)
+        lax.fori_loop(0, NT // 8, gradients, 0, unroll=8)
 
     lane = lax.broadcasted_iota(jnp.int32, (TR, 128), 1)
     placed = doubled(order[...], grads[...])
@@ -461,15 +462,21 @@
 def sweep_kernel(red, steps, out, steps_out):
     steps_out[...] = steps[...]
     rank = lax.axis_index("cells") * NX + lax.axis_index("tm")
-    shape = (32, 128)
+    shape = (24, 128)
     row = lax.broadcasted_iota(jnp.int32, shape, 0)
     lane = lax.broadcasted_iota(jnp.int32, shape, 1)
     k = lane % KB
-    beyond = ((row == 7) & (rank == 0)) | ((row == 24) & (rank == DEV - 1))
+    beyond = ((row == 23) & (rank == 0)) | ((row == 16) & (rank == DEV - 1))
     valid = jnp.where(beyond, 0.0, 1.0)
+    last = lax.broadcasted_iota(jnp.int32, (8, 128), 0) == 7
+
+    def loaded(r):
+        return jnp.concatenate([red[r, 8:24], jnp.where(last, red[r, 0:8], red[r, 24:32])], axis=0)
+
+    comps = [loaded(r) for r in range(6)]
     ahead, behind = {}, {}
     for n in range(10):
-        comp = red[n % 5]
+        comp = comps[n % 5]
         start = (n // 5) * 64
         for t in range(4):
             value = jnp.take_along_axis(comp, start + t * 16 + k, axis=1)
@@ -480,7 +487,7 @@
     for n, (i, j) in enumerate(PAIRS):
         if i == j:
             ahead[n, 0] = ahead[n, 0] + 34.0
-    fold = red[5]
+    fold = comps[5]
     fold = fold + pltpu.roll(fold, 64, 1)
     gradient = [jnp.take_along_axis(fold, m * KB + k, axis=1) for m in range(4)]
 
@@ -501,14 +508,14 @@
                     acc = acc + ahead[p, t] * up[t] + behind[p, t] * down[t]
                 misfit[m] = misfit[m] - acc
             before = jnp.where(k == 0, pltpu.roll(down[1], 1, 0), down[1])
-            after = jnp.where(k == KB - 1, pltpu.roll(up[1], 31, 0), up[1])
+            after = jnp.where(k == KB - 1, pltpu.roll(up[1], 23, 0), up[1])
             misfit[n] = misfit[n] + 16.0 * (before + after)
         x = [(v + 0.5 * w) * valid for v, w in zip(x, substitute(lower, inverse, misfit, 4))]
     sub8 = lax.broadcasted_iota(jnp.int32, (8, 128), 0)
     keep = sub8 == lax.broadcasted_iota(jnp.int32, (8, 128), 1) // KB
     for m in range(4):
         for h in range(2):
-            part = jnp.where(keep, x[m][8 + h * 8:16 + h * 8], 0.0)
+            part = jnp.where(keep, x[m][h * 8:8 + h * 8], 0.0)
             out[m:m + 1, h * 128:(h + 1) * 128] = jnp.sum(part, axis=0, keepdims=True)
 
 
@@ -527,7 +534,8 @@
         in_specs=[SMEM, SMEM, SMEM] + [VMEM] * 6,
         out_specs=(VMEM, VMEM),
         scratch_shapes=[
-            pltpu.VMEM((NC, NZ, NY * NX, 8, 128), f32),
+            pltpu.VMEM((NC * NZ, NY * NX, 8, 128), f32),
+            pltpu.SMEM((4, TR), jnp.int32),
             pltpu.VMEM((10 * TR, 128), f32),
             pltpu.VMEM((8 * TR, 128), f32),
             pltpu.VMEM((TR, 128), jnp.int32),

time: 59.4 us -> 56.8 us (0.956)
  Pallas kernels: 58.6 us -> 56.1 us
    pallas_call x1, Pallas kernels: 55.2 us -> 53 us  [per_device(): pl.pallas_call(main_kernel, out_shape=(jax.ShapeDtypeStruct((5, CELLS_HER...]
where the time goes in v6:
time: 56.8 us; the launch traced here: 56.7 us
  Pallas kernels  56.1 us (99%)
  between operations  0.64 us (1%)
    pallas_call x1, Pallas kernels, per_device(): pl.pallas_call(main_kernel, out_shape=(jax.ShapeDtypeStruct((5, CELLS_HER...  53 us
    pallas_call x1, Pallas kernels, per_device(): pl.pallas_call(sweep_kernel, out_shape=(jax.ShapeDtypeStruct((4, 256), f3...  3.01 us

profile of v6, /device:TPU:1, one launch (start us, length us, event | category | flops | bytes accessed | tf_op | source)
XLA Modules:
  0.0 56.7 jit_solution(13939138774903591566)
XLA Ops:
  0.6 53.0 %exchange.1 = (f32[5,512]{1,0:T(8,128)}, f32[6,32,128]{2,1,0:T(8,128)}) custom-call(s32[4]{0:T(128)} %counts.1, s32[4,64]{1,0:T(4,128)} %bitcast.1, s32[4,64]{1,0:T(4,128)} %slots.1, f32[4,256]{1,0:T(4,128)} %att_in.1, f32[5,64,512]{2,1,0:T(8,128)} %star.1, f32[4,64,512]{2,1,0:T(8,128)} %axis.1, f32[64,512]{1,0:T(8,128)} %observed.1, f32[64,512]{1,0:T(8,128)} %phase.1, ...), custom_call_target="tpu_custom_call" | custom-call | tf_op jit(solution)/shard_map/exchange/pallas_call | solution.py:528
  53.7 3.0 %sweeps.1 = (f32[4,256]{1,0:T(4,128)}, f32[5,512]{1,0:T(8,128)}) custom-call(f32[6,32,128]{2,1,0:T(8,128)} %get-tuple-element.6.red, f32[5,512]{1,0:T(8,128)} %get-tuple-element.7.steps), custom_call_target="tpu_custom_call" | custom-call | tf_op jit(solution)/shard_map/sweeps/pallas_call | solution.py:570

commit v7 on v6

--- a/solution.py
+++ b/solution.py
@@ -150,7 +150,7 @@
     for cell in range(CELLS_HERE):
         lanes = slice(cell * CS, (cell + 1) * CS)
 
-        def prepare(g, acc, cell=cell, lanes=lanes):
+        def prepare(g, carry, cell=cell, lanes=lanes):
             rows = pl.ds(aligned(g * 8), 8)
             at = cell * NT + g * 8
             live = jnp.where(sub8 + g * 8 < counts[cell], 1.0, 0.0)
@@ -161,15 +161,9 @@
             for m in range(4):
                 parts[pl.ds(aligned(m * TR + at), 8), :] = axis[m, rows, lanes]
                 parts[pl.ds(aligned((4 + m) * TR + at), 8), :] = b[m]
-            for jj in range(8):
-                ownm[pl.ds(at + jj, 1), :] = jnp.full((1, 128), owners[cell, g * 8 + jj], jnp.int32)
-            p = [star[m, rows, lanes] * live for m in range(5)]
-            terms = [p[i] * p[j] for i in range(5) for j in range(i + 1)]
-            return tuple(s + term for s, term in zip(acc, terms))
-
-        acc = lax.fori_loop(0, NT // 8, prepare, tuple(jnp.zeros((8, 128), f32) for _ in range(15)))
-        for n in range(15):
-            sums[n:n + 1, lanes] = jnp.sum(acc[n], axis=0, keepdims=True)
+            return carry
+
+        lax.fori_loop(0, NT // 8, prepare, 0)
 
     def sides(at):
         gap = knot - jnp.broadcast_to(offs[pl.ds(at, 1), :], (16, 128))
@@ -214,6 +208,7 @@
                 slot = slots[lax.shift_right_logical(g, 1), (g & 1) * 32 + jj + e]
                 finish(at + e, slot, big[e * 32:(e + 1) * 32])
                 owner = owners[lax.shift_right_logical(g, 1), (g & 1) * 32 + jj + e]
+                ownm[pl.ds(at + e, 1), :] = jnp.full((1, 128), owner, jnp.int32)
                 found[0, at + e] = ((owner & 4) << 1) | lax.shift_right_logical(owner, 5)
                 found[1, at + e] = lax.shift_right_logical(owner & 24, 1) | (owner & 3)
                 found[2, at + e] = lax.shift_right_logical(slot & 8, 1)
@@ -301,6 +296,20 @@
         return carry
 
     lax.fori_loop(0, TR // 8, spreads, 0)
+
+    for cell in range(CELLS_HERE):
+        lanes = slice(cell * CS, (cell + 1) * CS)
+
+        def squares(g, acc, cell=cell, lanes=lanes):
+            rows = pl.ds(aligned(g * 8), 8)
+            live = jnp.where(sub8 + g * 8 < counts[cell], 1.0, 0.0)
+            p = [star[m, rows, lanes] * live for m in range(5)]
+            both = [p[i] * p[j] for i in range(5) for j in range(i + 1)]
+            return tuple(s + term for s, term in zip(acc, both))
+
+        acc = lax.fori_loop(0, NT // 8, squares, tuple(jnp.zeros((8, 128), f32) for _ in range(15)))
+        for n in range(15):
+            sums[n:n + 1, lanes] = jnp.sum(acc[n], axis=0, keepdims=True)
 
     def entry(i, j):
         n = i * (i + 1) // 2 + j

time: 56.8 us -> 56.7 us (level)
  no operation moved by 1% of the time
where the time goes in v7:
time: 56.7 us; the launch traced here: 56.5 us
  Pallas kernels  55.9 us (99%)
  between operations  0.64 us (1%)
    pallas_call x1, Pallas kernels, per_device(): pl.pallas_call(main_kernel, out_shape=(jax.ShapeDtypeStruct((5, CELLS_HER...  52.9 us
    pallas_call x1, Pallas kernels, per_device(): pl.pallas_call(sweep_kernel, out_shape=(jax.ShapeDtypeStruct((4, 256), f3...  3.01 us

profile of v7, /device:TPU:1, one launch (start us, length us, event | category | flops | bytes accessed | tf_op | source)
XLA Modules:
  0.0 56.5 jit_solution(2293648175983088163)
XLA Ops:
  0.6 52.9 %exchange.1 = (f32[5,512]{1,0:T(8,128)}, f32[6,32,128]{2,1,0:T(8,128)}) custom-call(s32[4]{0:T(128)} %counts.1, s32[4,64]{1,0:T(4,128)} %bitcast.1, s32[4,64]{1,0:T(4,128)} %slots.1, f32[4,256]{1,0:T(4,128)} %att_in.1, f32[5,64,512]{2,1,0:T(8,128)} %star.1, f32[4,64,512]{2,1,0:T(8,128)} %axis.1, f32[64,512]{1,0:T(8,128)} %observed.1, f32[64,512]{1,0:T(8,128)} %phase.1, ...), custom_call_target="tpu_custom_call" | custom-call | tf_op jit(solution)/shard_map/exchange/pallas_call | solution.py:537
  53.5 3.0 %sweeps.1 = (f32[4,256]{1,0:T(4,128)}, f32[5,512]{1,0:T(8,128)}) custom-call(f32[6,32,128]{2,1,0:T(8,128)} %get-tuple-element.6.red, f32[5,512]{1,0:T(8,128)} %get-tuple-element.7.steps), custom_call_target="tpu_custom_call" | custom-call | tf_op jit(solution)/shard_map/sweeps/pallas_call | solution.py:579
